TPU v7x, 512 devices: a whole 4x8x8 slice. The times are simulated.
512 devices in a mesh: tx: 32 (over x, z), ty: 16 (over y, core).
Axes of the slice: x: 4, y: 8, z: 8, core: 2. Of those that a mesh axis runs over, the one named last changes fastest.
Arguments:
- features: bfloat16 [2048, 128, 128], P(('tx', 'ty')), may hold values from -6 to 6
- occupancy: int32 [2048, 128], P(('tx', 'ty')), may hold values from 0 to 1, as said below
- neighbors: int32 [27, 2048], P(None, ('tx', 'ty')), may hold values from -1 to 2047, as said below
- point_voxel: int32 [524288], P(('tx', 'ty')), may hold values from 0 to 511, as said below
- conv_weight: bfloat16 [27, 128, 128], replicated, may hold values from -0.109375 to 0.109375
- head_weight: bfloat16 [16, 128], replicated, may hold values from -0.5 to 0.5
- teacher: bfloat16 [16, 524288], P(None, ('tx', 'ty')), may hold values from -15 to 15
Outputs:
- grad_features: bfloat16 [2048, 128, 128], P(('tx', 'ty'))
- grad_weight: float32 [27, 128, 128], replicated
Inputs may be any that keep to these rules, and one draw needn't show every extreme that they name: `occupancy`: every voxel of a slot that holds no active brick is 0; every active brick has one or more occupied voxels. A brick's global slot is 4 times its tile's index (tx index times the number of ty devices plus ty index) plus (2 i + j) + k for its place (i, j, k) in the tile's 2 x 2 x 1 grid of bricks. neighbors[o, b] is the global slot of the brick at brick offset o from b if that brick is active and b is active, else -1; neighbors[13, b] is b exactly when b is active. At most 3 bricks of a tile are active, and some tile has exactly 3. `point_voxel`: each entry is 128 s + v for an occupied voxel v of slot s of the point's own tile.
All inputs are finite; a program needn't handle non-finite values.
Results may differ from a plain program's by a relative error of at most 0.0052.
Values may be sent and summed in bfloat16 or wider, within the bound.
A program may use at most 64 MiB of HBM per device.

v0:
```python
import jax
import jax.numpy as jnp
from jax import lax
from jax.sharding import PartitionSpec as P

GX = 2
GY = 2
GZ = 1


def with_halo(cells, sides, width):
    for axis, dim in sides:
        count = lax.axis_size(axis)
        ends = count - 1
        head = lax.slice_in_dim(cells, 0, width, axis=dim)
        tail = lax.slice_in_dim(cells, cells.shape[dim] - width, cells.shape[dim], axis=dim)
        cells = jnp.concatenate(
            [
                lax.ppermute(tail, axis, [(i, (i + 1) % count) for i in range(ends)]),
                cells,
                lax.ppermute(head, axis, [((i + 1) % count, i) for i in range(ends)]),
            ],
            axis=dim,
        )
    return cells


def span_of(move, length):
    if move < 0:
        return (length - 1, length)
    if move == 0:
        return (0, length)
    return (0, 1)


def assemble_blocks(table, index):
    planes = []
    for move_x in (-1, 0, 1):
        columns = []
        for move_y in (-1, 0, 1):
            pieces = []
            for move_z in (-1, 0, 1):
                offset = 9 * (move_x + 1) + 3 * (move_y + 1) + (move_z + 1)
                start_x, stop_x = span_of(move_x, 4)
                start_y, stop_y = span_of(move_y, 4)
                start_z, stop_z = span_of(move_z, 8)
                window = table[:, start_x:stop_x, start_y:stop_y, start_z:stop_z, :]
                pieces.append(jnp.take(window, index[offset], axis=0))
            columns.append(jnp.concatenate(pieces, axis=3))
        planes.append(jnp.concatenate(columns, axis=2))
    return jnp.concatenate(planes, axis=1)


def plane_columns(padded, move_x, transpose):
    channels = padded.shape[-1]
    windows = []
    for move_y in (-1, 0, 1):
        for move_z in (-1, 0, 1):
            if transpose:
                anchor = (1 - move_x, 1 - move_y, 1 - move_z)
            else:
                anchor = (1 + move_x, 1 + move_y, 1 + move_z)
            window = padded[
                :,
                anchor[0] : anchor[0] + 4,
                anchor[1] : anchor[1] + 4,
                anchor[2] : anchor[2] + 8,
                :,
            ]
            windows.append(window.reshape(-1, channels))
    return jnp.concatenate(windows, axis=1)


def convolve(padded, weight, transpose):
    channels = padded.shape[-1]
    summed = jnp.zeros((padded.shape[0] * 128, channels), jnp.float32)
    for move_x in (-1, 0, 1):
        first = 9 * (move_x + 1)
        if transpose:
            matrix = jnp.concatenate([weight[first + inner].T for inner in range(9)], axis=0)
        else:
            matrix = weight[first : first + 9].reshape(9 * channels, channels)
        columns = plane_columns(padded, move_x, transpose)
        summed = summed + jnp.dot(columns, matrix, preferred_element_type=jnp.float32)
    return summed


def weight_terms(padded, gradient):
    channels = padded.shape[-1]
    flat_grad = gradient.reshape(-1, channels)
    terms = []
    for move_x in (-1, 0, 1):
        columns = plane_columns(padded, move_x, False)
        product = lax.dot_general(
            columns, flat_grad, (((0,), (0,)), ((), ())), preferred_element_type=jnp.float32
        )
        terms.append(product.reshape(9, channels, channels))
    return jnp.concatenate(terms, axis=0)


def silu_slope(value):
    logistic = jax.nn.sigmoid(value)
    return logistic * (1.0 + value * (1.0 - logistic))


def tile_gradient(pre, occupied, voxel_index, teacher_block, head_weight):
    channels = pre.shape[-1]
    occupied_cells = occupied[..., None]
    hidden = (jax.nn.silu(pre) * occupied_cells).astype(jnp.bfloat16)
    chosen = jnp.take(hidden.reshape(-1, channels), voxel_index, axis=0)
    logits = lax.dot_general(
        head_weight, chosen, (((1,), (1,)), ((), ())), preferred_element_type=jnp.float32
    )
    student = jnp.exp(logits)
    student = student / jnp.sum(student, axis=0, keepdims=True)
    target = jnp.exp(teacher_block.astype(jnp.float32))
    target = target / jnp.sum(target, axis=0, keepdims=True)
    slope_logits = student - target
    per_point = jnp.dot(
        slope_logits.T, head_weight.astype(jnp.float32), precision=lax.Precision.HIGHEST
    )
    per_voxel = (
        jnp.zeros((pre.shape[0] * 128, channels), jnp.float32).at[voxel_index].add(per_point)
    )
    return (per_voxel.reshape(pre.shape) * silu_slope(pre) * occupied_cells).astype(jnp.bfloat16)


def neighbourhood(block, neighbors, chosen_rows):
    slots = block.shape[0]
    channels = block.shape[2]
    brick_grid = block.reshape(GX, GY, GZ, 128, channels)
    extended = with_halo(brick_grid, (("tx", 0), ("ty", 1)), 1)
    table_size = (GX + 2) * (GY + 2) * GZ
    table = jnp.concatenate(
        [
            extended.reshape(table_size, 4, 4, 8, channels),
            jnp.zeros((1, 4, 4, 8, channels), jnp.bfloat16),
        ],
        axis=0,
    )
    chosen = jnp.take(neighbors, chosen_rows, axis=1)
    owner_tile = chosen // slots
    owner_x = owner_tile // lax.axis_size("ty")
    owner_y = owner_tile % lax.axis_size("ty")
    slot_place = chosen % slots
    row_i = slot_place // (GY * GZ) + (owner_x - lax.axis_index("tx")) * GX + 1
    row_j = slot_place // GZ % GY + (owner_y - lax.axis_index("ty")) * GY + 1
    layer_k = slot_place % GZ
    table_row = (row_i * (GY + 2) + row_j) * GZ + layer_k
    table_row = jnp.where(chosen < 0, table_size, table_row)
    return assemble_blocks(table, table_row)


def normalise_terms(local_terms):
    summed = lax.psum(local_terms, ("tx", "ty"))
    return summed / jnp.sqrt(jnp.mean(summed * summed) + 1e-06)


def on_device(features, occupancy, neighbors, point_voxel, conv_weight, head_weight, teacher):
    slots = features.shape[0]
    channels = features.shape[2]
    occupied = occupancy.astype(jnp.float32)
    masked = features * occupancy.astype(jnp.bfloat16)[..., None]
    chosen_rows = jnp.arange(slots, dtype=jnp.int32)
    padded_x = neighbourhood(masked, neighbors, chosen_rows)
    pre_rows = convolve(padded_x, conv_weight, False).reshape(-1, 128, channels)
    gradient = tile_gradient(pre_rows, occupied, point_voxel, teacher, head_weight)
    padded_g = neighbourhood(gradient, neighbors, chosen_rows)
    back_rows = convolve(padded_g, conv_weight, True).reshape(-1, 128, channels)
    grad_features = (back_rows * occupied[..., None]).astype(jnp.bfloat16)
    local_terms = weight_terms(padded_x, jnp.take(gradient, chosen_rows, axis=0))
    grad_weight = normalise_terms(local_terms)
    return (grad_features, grad_weight)


def solution(mesh):
    in_specs = (
        P(("tx", "ty"), None, None),
        P(("tx", "ty"), None),
        P(None, ("tx", "ty")),
        P(("tx", "ty")),
        P(),
        P(),
        P(None, ("tx", "ty")),
    )
    out_specs = (P(("tx", "ty"), None, None), P())
    return jax.shard_map(
        on_device, mesh=mesh, in_specs=in_specs, out_specs=out_specs, check_vma=False
    )
```

profile of v0, /device:TPU:1, one launch (start us, length us, event | category | flops | bytes accessed | tf_op | source)
XLA Modules:
  0.0 434.6 jit_solution(17471954738965862023)
XLA Ops:
  7.2 1.4 fusion.70
  8.6 1.0 broadcast_multiply_fusion
  9.7 4.8 %collective-permute-start = (bf16[1,2,1,128,128]{4,3,1,2,0:T(8,128)(2,1)S(1)}, bf16[1,2,1,128,128]{4,3,1,2,0:T(8,128)(2,1)S(1)}, u32[]{:S(2)}, u32[]{:S(2)}) collective-permute-start(bf16[1,2,1,128,128]{4,3,1,2,0:T(8,128)(2,1)S(1)} %get-tuple-element.183), channel_id=1, source_target_pairs={{0,16},{16,32},{32,48},{48,64},{64,80},{80,96},{96,112},{112,128},... | collective-permute-start | bytes 196616 | tf_op jit(solution)/shard_map/ppermute | solution.py:19
  14.5 1.3 collective-permute-start.1
  15.9 1.2 gather_fusion.2
  41.5 5.2 %collective-permute-start.3 = (bf16[4,1,1,128,128]{4,1,0,3,2:T(2,128)(2,1)S(1)}, bf16[4,1,1,128,128]{4,1,0,3,2:T(2,128)(2,1)S(1)}, u32[]{:S(2)}, u32[]{:S(2)}) collective-permute-start(bf16[4,1,1,128,128]{4,1,0,3,2:T(2,128)(2,1)S(1)} %get-tuple-element.171), channel_id=1, source_target_pairs={{1,0},{2,1},{3,2},{4,3},{5,4},{6,5},{7,6},{8,7},{9,8},{10,9},{11,1... | collective-permute-start | bytes 393224 | tf_op jit(solution)/shard_map/ppermute | solution.py:21
  46.7 2.1 collective-permute-start.2
  50.0 1.9 collective-permute-done.2
  51.9 0.9 pad_maximum_fusion.1
  70.2 1.1 fusion.63
  74.9 1.4 gather_fusion.29
  76.9 1.4 gather_fusion.28
  79.1 1.4 gather_fusion.27
  81.1 1.4 gather_fusion.26
  83.3 1.6 gather_fusion.25
  87.0 1.4 gather_fusion.23
  90.5 1.4 gather_fusion.21
  92.6 1.1 maximum_maximum_fusion.1
  98.7 3.2 gather_fusion
  102.3 1.4 fusion.11
  103.7 6.2 %scatter_custom_fusion = f32[512,128]{1,0:T(8,128)S(1)} fusion(s32[1024]{0:T(1024)} %get-tuple-element.185, f32[1024,128]{1,0:T(8,128)S(1)} %fusion.11, f32[]{:T(128)} %constant.230.clone.1), kind=kCustom, calls=%fused_computation.206 | custom fusion | flops 131072 | bytes 262656 | tf_op jit(solution)/shard_map/scatter-add | solution.py:123
  110.7 1.3 gather_fusion.1
  112.0 1.3 collective-permute-start.5
  113.3 5.5 %collective-permute-start.4 = (bf16[1,2,1,128,128]{4,3,1,2,0:T(8,128)(2,1)}, bf16[1,2,1,128,128]{4,3,1,2,0:T(8,128)(2,1)}, u32[]{:S(2)}, u32[]{:S(2)}) collective-permute-start(bf16[1,2,1,128,128]{4,3,1,2,0:T(8,128)(2,1)} %get-tuple-element.178), channel_id=1, source_target_pairs={{0,16},{16,32},{32,48},{48,64},{64,80},{80,96},{96,112},{112,128},... | collective-permute-start | bytes 196616 | tf_op jit(solution)/shard_map/ppermute | solution.py:19
  118.9 1.6 copy.169
  120.4 1.6 broadcast_select_fusion.2
  122.1 1.4 copy.168
  123.5 2.3 fusion.76
  128.1 0.9 pad_maximum_fusion.3
  129.1 1.9 collective-permute-start.7
  131.0 4.7 %collective-permute-start.6 = (bf16[4,1,1,128,128]{4,3,1,0,2:T(8,128)(2,1)S(1)}, bf16[4,1,1,128,128]{4,3,1,0,2:T(8,128)(2,1)S(1)}, u32[]{:S(2)}, u32[]{:S(2)}) collective-permute-start(bf16[4,1,1,128,128]{4,3,1,0,2:T(8,128)(2,1)S(1)} %get-tuple-element.168), channel_id=1, source_target_pairs={{0,1},{1,2},{2,3},{3,4},{4,5},{5,6},{6,7},{7,8},{8,9},{9,10},{10,1... | collective-permute-start | bytes 393224 | tf_op jit(solution)/shard_map/ppermute | solution.py:19
  135.7 1.3 pad_maximum_fusion
  137.6 0.9 pad_maximum_fusion.2
  157.6 1.0 fusion.61
  160.2 1.3 gather_fusion.56
  161.5 1.3 broadcast_select_fusion.18
  162.8 1.5 copy.232
  164.3 1.4 gather_fusion.55
  165.7 1.4 bitcast_select_fusion.10
  167.8 1.2 gather_fusion.54
  169.0 1.3 broadcast_select_fusion.19
  170.3 1.4 copy.236
  171.7 2.0 gather_fusion.53
  175.1 1.6 gather_fusion.52
  185.2 1.0 maximum_maximum_fusion.3
  192.0 230.9 %all-reduce.4.cloned.1.call-done = f32[27,128,128]{2,1,0:T(8,128)} async-done(((f32[27,128,128]{2,1,0:T(8,128)}), f32[27,128,128]{2,1,0:T(8,128)}) %all-reduce.4.cloned.1.call-update) | async-done | bytes 1769488 | tf_op jit(solution)/shard_map/psum | solution.py:155
  422.9 2.7 multiply_reduce_fusion
  426.3 1.4 broadcast_divide_fusion
  (542 shorter events, 98.6 us)
Async XLA Ops:
  7.2 94.7 %copy-start = (bf16[16,128]{1,0:T(8,128)(2,1)S(1)}, bf16[16,128]{1,0:T(8,128)(2,1)}, u32[]{:S(2)}) copy-start(bf16[16,128]{1,0:T(8,128)(2,1)} %param.30) | copy-start | bytes 12292
  7.2 18.7 %copy-start.3 = (bf16[27,128,128]{2,1,0:T(8,128)(2,1)S(1)}, bf16[27,128,128]{2,1,0:T(8,128)(2,1)}, u32[]{:S(2)}) copy-start(bf16[27,128,128]{2,1,0:T(8,128)(2,1)} %param.29) | copy-start | bytes 2654212
  7.2 415.7 %all-reduce.4.cloned.1.call-start = ((), (), s32[]{:S(2)}) async-start(), calls=%async_computation | async-start | bytes 3538944 | tf_op jit(solution)/shard_map/psum | solution.py:155
  8.6 119.1 %copy-start.52 = (f32[4,128]{1,0:T(4,128)}, f32[4,128]{1,0:T(4,128)S(1)}, u32[]{:S(2)}) copy-start(f32[4,128]{1,0:T(4,128)S(1)} %get-tuple-element.186) | copy-start | bytes 6148
  9.7 17.1 %copy-start.56 = (s32[1024]{0:T(1024)S(1)}, s32[1024]{0:T(1024)}, u32[]{:S(2)}) copy-start(s32[1024]{0:T(1024)} %param.28) | copy-start | bytes 12292
  9.7 31.0 %collective-permute-start = (bf16[1,2,1,128,128]{4,3,1,2,0:T(8,128)(2,1)S(1)}, bf16[1,2,1,128,128]{4,3,1,2,0:T(8,128)(2,1)S(1)}, u32[]{:S(2)}, u32[]{:S(2)}) collective-permute-start(bf16[1,2,1,128,128]{4,3,1,2,0:T(8,128)(2,1)S(1)} %get-tuple-element.183), channel_id=1, source_target_pairs={{0,16},{16,32},{32,48},{48,64},{64,80},{80,96},{96,112},{112,128},... | collective-permute-start | bytes 196616 | tf_op jit(solution)/shard_map/ppermute | solution.py:19
  14.5 26.5 %collective-permute-start.1 = (bf16[1,2,1,128,128]{4,3,1,2,0:T(8,128)(2,1)S(1)}, bf16[1,2,1,128,128]{4,3,1,2,0:T(8,128)(2,1)S(1)}, u32[]{:S(2)}, u32[]{:S(2)}) collective-permute-start(bf16[1,2,1,128,128]{4,3,1,2,0:T(8,128)(2,1)S(1)} %get-tuple-element.182), channel_id=1, source_target_pairs={{16,0},{32,16},{48,32},{64,48},{80,64},{96,80},{112,96},{128,112},... | collective-permute-start | bytes 196616 | tf_op jit(solution)/shard_map/ppermute | solution.py:21
  15.8 10.1 %copy-start.102 = (pred[4]{0:T(512)(128)(4,1)}, pred[4]{0:T(512)(128)(4,1)S(1)}, u32[]{:S(2)}) copy-start(pred[4]{0:T(512)(128)(4,1)S(1)} %broadcast_compare_fusion) | copy-start | bytes 16
  15.8 10.0 %copy-start.61 = (s32[1024]{0:T(1024)}, s32[1024]{0:T(1024)S(1)}, u32[]{:S(2)}) copy-start(s32[1024]{0:T(1024)S(1)} %pad_clamp_fusion.27) | copy-start | bytes 12292
  18.6 40.8 %copy-start.76 = (pred[4]{0:T(512)(128)(4,1)}, pred[4]{0:T(512)(128)(4,1)S(1)}, u32[]{:S(2)}) copy-start(pred[4]{0:T(512)(128)(4,1)S(1)} %get-tuple-element.231) | copy-start | bytes 16
  19.2 41.6 %copy-start.74 = (pred[4]{0:T(512)(128)(4,1)}, pred[4]{0:T(512)(128)(4,1)S(1)}, u32[]{:S(2)}) copy-start(pred[4]{0:T(512)(128)(4,1)S(1)} %get-tuple-element.233) | copy-start | bytes 16
  19.7 36.1 %copy-start.70 = (pred[4]{0:T(512)(128)(4,1)}, pred[4]{0:T(512)(128)(4,1)S(1)}, u32[]{:S(2)}) copy-start(pred[4]{0:T(512)(128)(4,1)S(1)} %get-tuple-element.235) | copy-start | bytes 16
  22.5 34.9 %copy-start.82 = (pred[4]{0:T(512)(128)(4,1)}, pred[4]{0:T(512)(128)(4,1)S(1)}, u32[]{:S(2)}) copy-start(pred[4]{0:T(512)(128)(4,1)S(1)} %get-tuple-element.242) | copy-start | bytes 16
  23.1 35.0 %copy-start.79 = (pred[4]{0:T(512)(128)(4,1)}, pred[4]{0:T(512)(128)(4,1)S(1)}, u32[]{:S(2)}) copy-start(pred[4]{0:T(512)(128)(4,1)S(1)} %get-tuple-element.245) | copy-start | bytes 16
  23.6 33.0 %copy-start.90 = (pred[4]{0:T(512)(128)(4,1)}, pred[4]{0:T(512)(128)(4,1)S(1)}, u32[]{:S(2)}) copy-start(pred[4]{0:T(512)(128)(4,1)S(1)} %get-tuple-element.220) | copy-start | bytes 16
  27.9 29.6 %copy-start.66 = (s32[1024]{0:T(1024)}, s32[1024]{0:T(1024)S(1)}, u32[]{:S(2)}) copy-start(s32[1024]{0:T(1024)S(1)} %get-tuple-element.219) | copy-start | bytes 12292
  28.5 29.7 %copy-start.65 = (s32[1024]{0:T(1024)}, s32[1024]{0:T(1024)S(1)}, u32[]{:S(2)}) copy-start(s32[1024]{0:T(1024)S(1)} %get-tuple-element.202) | copy-start | bytes 12292
  28.5 30.3 %copy-start.60 = (s32[1024]{0:T(1024)}, s32[1024]{0:T(1024)S(1)}, u32[]{:S(2)}) copy-start(s32[1024]{0:T(1024)S(1)} %get-tuple-element.203) | copy-start | bytes 12292
  28.5 31.0 %copy-start.64 = (s32[1024]{0:T(1024)}, s32[1024]{0:T(1024)S(1)}, u32[]{:S(2)}) copy-start(s32[1024]{0:T(1024)S(1)} %get-tuple-element.204) | copy-start | bytes 12292
  28.6 31.6 %copy-start.59 = (s32[1024]{0:T(1024)}, s32[1024]{0:T(1024)S(1)}, u32[]{:S(2)}) copy-start(s32[1024]{0:T(1024)S(1)} %get-tuple-element.205) | copy-start | bytes 12292
  28.6 32.4 %copy-start.58 = (s32[1024]{0:T(1024)}, s32[1024]{0:T(1024)S(1)}, u32[]{:S(2)}) copy-start(s32[1024]{0:T(1024)S(1)} %get-tuple-element.206) | copy-start | bytes 12292
  29.2 26.0 %copy-start.57 = (s32[1024]{0:T(1024)}, s32[1024]{0:T(1024)S(1)}, u32[]{:S(2)}) copy-start(s32[1024]{0:T(1024)S(1)} %get-tuple-element.207) | copy-start | bytes 12292
  29.8 26.2 %copy-start.63 = (s32[1024]{0:T(1024)}, s32[1024]{0:T(1024)S(1)}, u32[]{:S(2)}) copy-start(s32[1024]{0:T(1024)S(1)} %get-tuple-element.210) | copy-start | bytes 12292
  31.6 25.2 %copy-start.62 = (s32[1024]{0:T(1024)}, s32[1024]{0:T(1024)S(1)}, u32[]{:S(2)}) copy-start(s32[1024]{0:T(1024)S(1)} %get-tuple-element.216) | copy-start | bytes 12292
  36.7 12.7 %copy-start.48 = (bf16[16,1024]{1,0:T(8,128)(2,1)S(1)}, bf16[16,1024]{1,0:T(8,128)(2,1)}, u32[]{:S(2)}) copy-start(bf16[16,1024]{1,0:T(8,128)(2,1)} %param.31) | copy-start | bytes 98308
  40.0 12.8 %copy-start.38 = (bf16[1152,128]{0,1:T(8,128)(2,1)}, bf16[1152,128]{0,1:T(8,128)(2,1)S(1)}, u32[]{:S(2)}) copy-start(bf16[1152,128]{0,1:T(8,128)(2,1)S(1)} %get-tuple-element.38) | copy-start | bytes 884740
  40.0 12.8 %copy-start.40 = (bf16[1152,128]{0,1:T(8,128)(2,1)}, bf16[1152,128]{0,1:T(8,128)(2,1)S(1)}, u32[]{:S(2)}) copy-start(bf16[1152,128]{0,1:T(8,128)(2,1)S(1)} %get-tuple-element.39) | copy-start | bytes 884740
  40.0 12.8 %copy-start.42 = (bf16[1152,128]{0,1:T(8,128)(2,1)}, bf16[1152,128]{0,1:T(8,128)(2,1)S(1)}, u32[]{:S(2)}) copy-start(bf16[1152,128]{0,1:T(8,128)(2,1)S(1)} %get-tuple-element.40) | copy-start | bytes 884740
  41.5 8.6 %collective-permute-start.3 = (bf16[4,1,1,128,128]{4,1,0,3,2:T(2,128)(2,1)S(1)}, bf16[4,1,1,128,128]{4,1,0,3,2:T(2,128)(2,1)S(1)}, u32[]{:S(2)}, u32[]{:S(2)}) collective-permute-start(bf16[4,1,1,128,128]{4,1,0,3,2:T(2,128)(2,1)S(1)} %get-tuple-element.171), channel_id=1, source_target_pairs={{1,0},{2,1},{3,2},{4,3},{5,4},{6,5},{7,6},{8,7},{9,8},{10,9},{11,1... | collective-permute-start | bytes 393224 | tf_op jit(solution)/shard_map/ppermute | solution.py:21
  46.7 5.2 %collective-permute-start.2 = (bf16[4,1,1,128,128]{4,1,0,3,2:T(2,128)(2,1)S(1)}, bf16[4,1,1,128,128]{4,1,0,3,2:T(2,128)(2,1)S(1)}, u32[]{:S(2)}, u32[]{:S(2)}) collective-permute-start(bf16[4,1,1,128,128]{4,1,0,3,2:T(2,128)(2,1)S(1)} %get-tuple-element.170), channel_id=1, source_target_pairs={{0,1},{1,2},{2,3},{3,4},{4,5},{5,6},{6,7},{7,8},{8,9},{9,10},{10,1... | collective-permute-start | bytes 393224 | tf_op jit(solution)/shard_map/ppermute | solution.py:19
  56.8 8.7 %copy-start.84 = (pred[4]{0:T(512)(128)(4,1)S(1)}, pred[4]{0:T(512)(128)(4,1)}, u32[]{:S(2)}) copy-start(pred[4]{0:T(512)(128)(4,1)} %get-tuple-element.239) | copy-start | bytes 16
  56.8 9.4 %copy-start.83 = (pred[4]{0:T(512)(128)(4,1)S(1)}, pred[4]{0:T(512)(128)(4,1)}, u32[]{:S(2)}) copy-start(pred[4]{0:T(512)(128)(4,1)} %get-tuple-element.240) | copy-start | bytes 16
  57.4 9.6 %copy-start.67 = (pred[4]{0:T(512)(128)(4,1)S(1)}, pred[4]{0:T(512)(128)(4,1)}, u32[]{:S(2)}) copy-start(pred[4]{0:T(512)(128)(4,1)} %get-tuple-element.241) | copy-start | bytes 16
  57.5 10.2 %copy-start.81 = (pred[4]{0:T(512)(128)(4,1)S(1)}, pred[4]{0:T(512)(128)(4,1)}, u32[]{:S(2)}) copy-start(pred[4]{0:T(512)(128)(4,1)} %get-tuple-element.243) | copy-start | bytes 16
  57.5 11.0 %copy-start.80 = (pred[4]{0:T(512)(128)(4,1)S(1)}, pred[4]{0:T(512)(128)(4,1)}, u32[]{:S(2)}) copy-start(pred[4]{0:T(512)(128)(4,1)} %get-tuple-element.244) | copy-start | bytes 16
  59.5 10.4 %copy-start.37 = (bf16[4,4,1,8,128]{4,3,2,1,0:T(8,128)(2,1)}, bf16[4,4,1,8,128]{4,3,2,1,0:T(8,128)(2,1)S(1)}, u32[]{:S(2)}) copy-start(bf16[4,4,1,8,128]{4,3,2,1,0:T(8,128)(2,1)S(1)} %bitcast_select_fusion.5) | copy-start | bytes 98308
  60.2 9.7 %copy-start.47 = (bf16[4,4,1,1,128]{4,3,2,1,0:T(2,128)(2,1)}, bf16[4,4,1,1,128]{4,3,2,1,0:T(2,128)(2,1)S(1)}, u32[]{:S(2)}) copy-start(bf16[4,4,1,1,128]{4,3,2,1,0:T(2,128)(2,1)S(1)} %broadcast_select_fusion.15) | copy-start | bytes 12292
  98.5 11.3 %copy-start.10 = (f32[512,128]{1,0:T(8,128)}, f32[512,128]{1,0:T(8,128)S(1)}, u32[]{:S(2)}) copy-start(f32[512,128]{1,0:T(8,128)S(1)} %get-tuple-element.190) | copy-start | bytes 786436
  109.9 9.0 %copy-start.5 = (f32[512,128]{1,0:T(8,128)}, f32[512,128]{1,0:T(8,128)S(1)}, u32[]{:S(2)}) copy-start(f32[512,128]{1,0:T(8,128)S(1)} %scatter_custom_fusion) | copy-start | bytes 786436
  112.0 16.1 %collective-permute-start.5 = (bf16[1,2,1,128,128]{4,3,1,0,2:T(8,128)(2,1)}, bf16[1,2,1,128,128]{4,3,1,0,2:T(8,128)(2,1)}, u32[]{:S(2)}, u32[]{:S(2)}) collective-permute-start(bf16[1,2,1,128,128]{4,3,1,0,2:T(8,128)(2,1)} %get-tuple-element.179), channel_id=1, source_target_pairs={{16,0},{32,16},{48,32},{64,48},{80,64},{96,80},{112,96},{128,112},... | collective-permute-start | bytes 196616 | tf_op jit(solution)/shard_map/ppermute | solution.py:21
  113.3 14.8 %collective-permute-start.4 = (bf16[1,2,1,128,128]{4,3,1,2,0:T(8,128)(2,1)}, bf16[1,2,1,128,128]{4,3,1,2,0:T(8,128)(2,1)}, u32[]{:S(2)}, u32[]{:S(2)}) collective-permute-start(bf16[1,2,1,128,128]{4,3,1,2,0:T(8,128)(2,1)} %get-tuple-element.178), channel_id=1, source_target_pairs={{0,16},{16,32},{32,48},{48,64},{64,80},{80,96},{96,112},{112,128},... | collective-permute-start | bytes 196616 | tf_op jit(solution)/shard_map/ppermute | solution.py:19
  127.7 8.0 %copy-start.4 = (f32[9,128,128]{2,1,0:T(8,128)S(1)}, f32[9,128,128]{2,1,0:T(8,128)}, u32[]{:S(2)}) copy-start(f32[9,128,128]{2,1,0:T(8,128)} %fusion.76) | copy-start | bytes 1769476
  129.1 8.0 %collective-permute-start.7 = (bf16[4,1,1,128,128]{4,3,1,0,2:T(8,128)(2,1)S(1)}, bf16[4,1,1,128,128]{4,3,1,0,2:T(8,128)(2,1)S(1)}, u32[]{:S(2)}, u32[]{:S(2)}) collective-permute-start(bf16[4,1,1,128,128]{4,3,1,0,2:T(8,128)(2,1)S(1)} %get-tuple-element.169), channel_id=1, source_target_pairs={{1,0},{2,1},{3,2},{4,3},{5,4},{6,5},{7,6},{8,7},{9,8},{10,9},{11,1... | collective-permute-start | bytes 393224 | tf_op jit(solution)/shard_map/ppermute | solution.py:21
  131.0 6.6 %collective-permute-start.6 = (bf16[4,1,1,128,128]{4,3,1,0,2:T(8,128)(2,1)S(1)}, bf16[4,1,1,128,128]{4,3,1,0,2:T(8,128)(2,1)S(1)}, u32[]{:S(2)}, u32[]{:S(2)}) collective-permute-start(bf16[4,1,1,128,128]{4,3,1,0,2:T(8,128)(2,1)S(1)} %get-tuple-element.168), channel_id=1, source_target_pairs={{0,1},{1,2},{2,3},{3,4},{4,5},{5,6},{6,7},{7,8},{8,9},{9,10},{10,1... | collective-permute-start | bytes 393224 | tf_op jit(solution)/shard_map/ppermute | solution.py:19
  141.8 8.2 %copy-start.93 = (pred[4]{0:T(512)(128)(4,1)S(1)}, pred[4]{0:T(512)(128)(4,1)}, u32[]{:S(2)}) copy-start(pred[4]{0:T(512)(128)(4,1)} %get-tuple-element.230) | copy-start | bytes 16
  141.9 9.0 %copy-start.77 = (pred[4]{0:T(512)(128)(4,1)S(1)}, pred[4]{0:T(512)(128)(4,1)}, u32[]{:S(2)}) copy-start(pred[4]{0:T(512)(128)(4,1)} %copy-done.76) | copy-start | bytes 16
  141.9 9.8 %copy-start.89 = (pred[4]{0:T(512)(128)(4,1)S(1)}, pred[4]{0:T(512)(128)(4,1)}, u32[]{:S(2)}) copy-start(pred[4]{0:T(512)(128)(4,1)} %get-tuple-element.232) | copy-start | bytes 16
  141.9 10.6 %copy-start.75 = (pred[4]{0:T(512)(128)(4,1)S(1)}, pred[4]{0:T(512)(128)(4,1)}, u32[]{:S(2)}) copy-start(pred[4]{0:T(512)(128)(4,1)} %copy-done.74) | copy-start | bytes 16
  (68 other events, 170.0 us)
Sparse Core Ops, SparseCore 0:
  137.1 285.7 all-reduce.3
where the time goes:
time: 437 us; the launch traced here: 435 us
  waiting for transfers between devices  233 us (53%)
  local copies, waits for them, and re-layouts  91.5 us (21%)
  other arithmetic  57.9 us (13%)
  starting transfers between devices  26.9 us (6%)
  between operations  17.1 us (4%)
  matrix products  7.81 us (2%)
    psum x1, waiting for transfers between devices, normalise_terms(): summed = lax.psum(local_terms, ('tx', 'ty'))  231 us
    gather x54, local copies, waits for them, and re-layouts, assemble_blocks(): pieces.append(jnp.take(window, index[offset], axis=0))  45.3 us
    select_n x81, other arithmetic, assemble_blocks(): pieces.append(jnp.take(window, index[offset], axis=0))  17.6 us
    ppermute x4, starting transfers between devices, with_halo(): lax.ppermute(tail, axis, [(i, (i + 1) % count) for i in range(ends)])  17.1 us
    unnamed x282, local copies, waits for them, and re-layouts  15.3 us
    ppermute x4, starting transfers between devices, with_halo(): lax.ppermute(head, axis, [((i + 1) % count, i) for i in range(ends)])  9.72 us
  transfers between devices with their start and end apart: 9, of which 3 were waited for; matrix products, arithmetic and copies ran while one was open for 20% of the time, Pallas kernels for 0%

commit v1 on v0

v1 whole, which is shorter than its diff:
```python
import functools

import jax
import jax.numpy as jnp
from jax import lax
from jax.experimental import pallas as pl
from jax.experimental.pallas import tpu as pltpu
from jax.sharding import PartitionSpec as P

F32 = jnp.float32
BF16 = jnp.bfloat16
MESH = pl.DeviceIdType.MESH
ROUTES = ((-1, 0), (1, 0), (0, -1), (0, 1), (-1, -1), (-1, 1), (1, -1), (1, 1))
HALF = 14
TN = (((0,), (0,)), ((), ()))
NT = (((1,), (1,)), ((), ()))


def span_to_send(step):
    if step < 0:
        return slice(1, 2)
    if step > 0:
        return slice(8, 9)
    return slice(1, 9)


def span_received(step):
    if step < 0:
        return slice(9, 10)
    if step > 0:
        return slice(0, 1)
    return slice(1, 9)


def split3(value):
    one = value.astype(BF16)
    rest = value - one.astype(F32)
    two = rest.astype(BF16)
    three = (rest - two.astype(F32)).astype(BF16)
    return one, two, three


def kernel(
    sizes,
    near_ref, occ_ref, feat_ref, point_ref, weight_hbm, head_ref, teacher_ref,
    grad_ref, sum_ref, norm_ref,
    cells, occ_cells, columns, columns_g, weight, weight_t, halo_out, halo_in,
    terms, pair_out, pair_in, ring_out, ring_in, mid, mid_in, row_out, row_in, last, full,
    weight_sem, halo_send, halo_recv, pair_send, pair_recv, ring_send, ring_recv,
    mid_send, mid_recv, row_send, row_recv, thin_send, thin_recv,
    wide_send, wide_recv, core_send, core_recv,
):
    nx, ring, per, used = sizes
    rows = 64 // ring
    n_tx = nx * ring
    n_ty = 2 * ring
    tx = lax.axis_index("tx")
    ty = lax.axis_index("ty")
    place_x, place_z = tx // ring, tx % ring
    place_y, core = ty // 2, ty % 2

    def along_x(d):
        return (((place_x + d) % nx) * ring + place_z, ty)

    def along_z(d):
        return (place_x * ring + (place_z + d) % ring, ty)

    def along_y(d):
        return (tx, ((place_y + d) % ring) * 2 + core)

    partner = (tx, place_y * 2 + 1 - core)
    first_peer = (along_y, along_z)
    second_peer = (along_z, along_y)
    first_place = (place_y, place_z)
    second_place = (place_z, place_y)

    def toward(route):
        ex, ey = route
        return ((tx + ex + n_tx) % n_tx, (ty + ey + n_ty) % n_ty)

    def remote(src, dst, send, recv, device):
        return pltpu.make_async_remote_copy(
            src_ref=src, dst_ref=dst, send_sem=send, recv_sem=recv,
            device_id=device, device_id_type=MESH,
        )

    weight_copy = pltpu.make_async_copy(weight_hbm, weight, weight_sem)
    weight_copy.start()

    barrier = pltpu.get_barrier_semaphore()

    def greet(device):
        pl.semaphore_signal(barrier, inc=1, device_id=device, device_id_type=MESH)

    for route in ROUTES:
        greet(toward(route))
    greet(partner)
    for d in range(1, ring):
        greet(along_y(d))
        greet(along_z(d))
    for d in range(1, nx):
        greet(along_x(d))

    for slot in range(4):
        i, j = slot // 2, slot % 2
        active = (near_ref[13, slot] >= 0).astype(jnp.int32)
        row = (occ_ref[slot : slot + 1, :] * active).astype(F32)
        column = jnp.broadcast_to(row, (128, 128)).T
        occ_cells[4 * i : 4 * i + 4, 4 * j : 4 * j + 4] = column.reshape(4, 4, 8, 128)
        masked = feat_ref[slot].astype(F32) * column
        cells[1 + 4 * i : 5 + 4 * i, 1 + 4 * j : 5 + 4 * j] = masked.reshape(4, 4, 8, 128)

    def halo_copy(turn, index):
        count = 64 if index < 4 else 16
        return remote(
            halo_out.at[turn, index, 0:count], halo_in.at[turn, index, 0:count],
            halo_send.at[turn, index], halo_recv.at[turn, index], toward(ROUTES[index]),
        )

    def stage_halo(turn):
        for index, (ex, ey) in enumerate(ROUTES):
            block = cells[span_to_send(ex), span_to_send(ey)]
            if index < 4:
                halo_out[turn, index] = block.reshape(64, 128).astype(BF16)
            else:
                block = block.reshape(8, 128)
                halo_out[turn, index, 0:16] = jnp.concatenate([block, block], axis=0).astype(BF16)

    def send_halo(turn):
        for index in (4, 5, 6, 7, 0, 1, 2, 3):
            halo_copy(turn, index).start()

    def take_halo(turn):
        for index, (ex, ey) in enumerate(ROUTES):
            halo_copy(turn, index).wait_recv()
            from_x, from_y = tx - ex, ty - ey
            inside = (from_x >= 0) & (from_x < n_tx) & (from_y >= 0) & (from_y < n_ty)
            keep = inside.astype(jnp.int32).astype(F32)
            if index < 4:
                block = halo_in[turn, index].astype(F32) * keep
                shape = (1, 8, 8, 128) if ex else (8, 1, 8, 128)
            else:
                block = halo_in[turn, index, 0:16].astype(F32)[0:8] * keep
                shape = (1, 1, 8, 128)
            cells[span_received(ex), span_received(ey)] = block.reshape(shape)

    layer = lax.broadcasted_iota(jnp.int32, (80, 8, 128), 1)

    def fill_columns(target, flip):
        for dy in range(3):
            start = 2 - dy if flip else dy
            block = cells[:, start : start + 8].reshape(80, 8, 128)
            for dz in range(3):
                move = 1 - dz if flip else dz - 1
                if move > 0:
                    shifted = jnp.where(layer == 7, 0.0, pltpu.roll(block, 7, 1))
                elif move < 0:
                    shifted = jnp.where(layer == 0, 0.0, pltpu.roll(block, 1, 1))
                else:
                    shifted = block
                lane = 128 * (3 * dy + dz)
                target[:, lane : lane + 128] = shifted.reshape(640, 128).astype(BF16)

    stage_halo(0)
    pl.semaphore_wait(barrier, 9 + 2 * (ring - 1) + nx - 1)
    send_halo(0)

    teacher = jnp.exp(teacher_ref[...].astype(F32))
    target = teacher / jnp.sum(teacher, axis=0, keepdims=True)
    where = point_ref[...]
    spread = (
        (where // 256) * 256 + (where // 32) % 4 * 64
        + (where // 128) % 2 * 32 + where % 32
    )
    voxel = lax.broadcasted_iota(jnp.int32, (512, 1024), 0)
    hits = jnp.where(voxel == spread, 1.0, 0.0).astype(BF16)
    parts = jnp.concatenate([*split3(target), jnp.ones((16, 1024), BF16)], axis=0)
    sums = lax.dot_general(parts, hits, NT, preferred_element_type=F32)
    target_sum = sums[0:16] + (sums[16:32] + sums[32:48])
    points = sums[48:64]

    weight_copy.wait()
    for k in range(27):
        lane = 128 * (k % 9)
        weight_t[k // 9, :, lane : lane + 128] = weight[k]

    take_halo(0)
    fill_columns(columns, False)

    pre = jnp.zeros((512, 128), F32)
    for q in range(3):
        pre += jnp.dot(
            columns[64 * q : 64 * q + 512, :],
            weight[9 * q : 9 * q + 9].reshape(1152, 128),
            preferred_element_type=F32,
        )
    occupied = occ_cells[...].reshape(512, 128)
    logistic = 1.0 / (1.0 + jnp.exp(-pre))
    hidden = (pre * logistic * occupied).astype(BF16)
    slope = logistic * (1.0 + pre * (1.0 - logistic)) * occupied

    logits = lax.dot_general(head_ref[...], hidden, NT, preferred_element_type=F32)
    student = jnp.exp(logits)
    student = student / jnp.sum(student, axis=0, keepdims=True)
    slope_logits = jnp.where(points > 0.0, points * student - target_sum, 0.0)
    head3 = jnp.concatenate([head_ref[...]] * 3, axis=0)
    pieces = jnp.concatenate(split3(slope_logits), axis=0)
    dhidden = lax.dot_general(pieces, head3, TN, preferred_element_type=F32)
    dpre = (dhidden * slope).astype(BF16)

    cells[1:9, 1:9] = dpre.astype(F32).reshape(8, 8, 8, 128)
    stage_halo(1)
    send_halo(1)

    for q in range(3):
        term = lax.dot_general(
            columns[64 * q : 64 * q + 512, :], dpre, TN, preferred_element_type=F32
        )
        terms[9 * q : 9 * q + 9] = term.reshape(9, 128, 128)
    terms[27:28] = jnp.zeros((1, 128, 128), F32)

    def pair_copy(h, q):
        return remote(
            pair_out.at[h, q], pair_in.at[h, q],
            pair_send.at[h, q], pair_recv.at[h, q], partner,
        )

    def own_rows(which, q):
        return pl.ds(pl.multiple_of(which * 64 + q * rows, rows), rows)

    def pair_step(d, carry):
        for h in range(2):
            q = (first_place[h] + d) % ring
            value = terms[HALF * h : HALF * h + HALF, own_rows(1 - core, q), :]
            pair_out[h, q] = value.reshape(HALF * rows, 128).astype(BF16)
            pair_copy(h, q).start()
        return carry

    lax.fori_loop(1, ring + 1, pair_step, 0)

    take_halo(1)
    fill_columns(columns_g, True)

    def ring_copy(h, d):
        return remote(
            ring_out.at[h, d], ring_in.at[h, d],
            ring_send.at[h, d], ring_recv.at[h, d], first_peer[h](d),
        )

    def paired(h, q):
        pair_copy(h, q).wait_recv()
        own = terms[HALF * h : HALF * h + HALF, own_rows(core, q), :]
        return own + pair_in[h, q].astype(F32).reshape(HALF, rows, 128)

    def ring_step(d, carry):
        for h in range(2):
            q = (first_place[h] + d) % ring
            ring_out[h, d] = paired(h, q).reshape(HALF * rows, 128).astype(BF16)
            ring_copy(h, d).start()
        return carry

    lax.fori_loop(1, ring, ring_step, 0)
    for h in range(2):
        mid[h, 0:HALF] = paired(h, first_place[h])
        if per * ring > HALF:
            mid[h, HALF : per * ring] = jnp.zeros((per * ring - HALF, rows, 128), F32)

    back = jnp.zeros((512, 128), F32)
    for q in range(3):
        back += lax.dot_general(
            columns_g[64 * (2 - q) : 64 * (2 - q) + 512, :], weight_t[q], NT,
            preferred_element_type=F32,
        )
    back = (back * occ_cells[...].reshape(512, 128)).reshape(8, 8, 8, 128)
    for slot in range(4):
        i, j = slot // 2, slot % 2
        block = back[4 * i : 4 * i + 4, 4 * j : 4 * j + 4]
        grad_ref[slot] = block.reshape(128, 128).astype(BF16)

    def ring_sum(d, carry):
        for h in range(2):
            ring_copy(h, d).wait_recv()
            mid[h, 0:HALF] += ring_in[h, d].astype(F32).reshape(HALF, rows, 128)
        return carry

    lax.fori_loop(1, ring, ring_sum, 0)

    def mid_copy(h, d):
        p = (second_place[h] + d) % ring
        return remote(
            mid.at[h, pl.ds(p * per, per)], mid_in.at[h, d],
            mid_send.at[h, d], mid_recv.at[h, d], second_peer[h](d),
        )

    def each_peer(action):
        def step(d, carry):
            for h in range(2):
                action(h, d)
            return carry

        lax.fori_loop(1, ring, step, 0)

    each_peer(lambda h, d: mid_copy(h, d).start())
    for h in range(2):
        row_out[h] = mid[h, pl.ds(second_place[h] * per, per)]

    def mid_sum(h, d):
        mid_copy(h, d).wait_recv()
        row_out[h] += mid_in[h, d]

    each_peer(mid_sum)

    def row_copy(d):
        return remote(
            row_out, row_in.at[place_x], row_send.at[d], row_recv.at[d], along_x(d)
        )

    for d in range(1, nx):
        row_copy(d).start()
    row_in[place_x] = row_out[...]
    for d in range(1, nx):
        row_copy(d).wait_recv()
    total = row_in[0]
    for x in range(1, nx):
        total += row_in[x]
    for h in range(2):
        final = total[h].reshape(per * rows, 128).astype(BF16)
        last[h] = final
        full[core, h, first_place[h], second_place[h]] = final

    def thin_copy(h, d):
        return remote(
            last.at[h], full.at[core, h, first_place[h], second_place[h]],
            thin_send.at[h, d], thin_recv.at[h, d], second_peer[h](d),
        )

    each_peer(lambda h, d: thin_copy(h, d).start())
    each_peer(lambda h, d: thin_copy(h, d).wait_recv())

    def wide_copy(h, d):
        block = full.at[core, h, first_place[h], 0:used]
        return remote(
            block, block, wide_send.at[h, d], wide_recv.at[h, d], first_peer[h](d)
        )

    def core_copy(h, q):
        block = full.at[core, h, q, 0:used]
        return remote(block, block, core_send.at[h, q], core_recv.at[h, q], partner)

    each_peer(lambda h, d: wide_copy(h, d).start())
    for h in range(2):
        core_copy(h, first_place[h]).start()

    def pass_on(h, d):
        wide_copy(h, d).wait_recv()
        core_copy(h, (first_place[h] + ring - d) % ring).start()

    each_peer(pass_on)

    def collect(q, squares):
        for h in range(2):
            core_copy(h, q).wait_recv()
            for side in range(2):
                block = full[side, h, q, 0:used].astype(F32).reshape(used * per, rows, 128)
                count = HALF if h == 0 else 27 - HALF
                block = block[0:count]
                sum_ref[HALF * h : HALF * h + count, own_rows(side, q), :] = block
                squares = squares + jnp.sum((block * block).reshape(-1, 8, 128), axis=0)
        return squares

    squares = lax.fori_loop(0, ring, collect, jnp.zeros((8, 128), F32))
    mean = jnp.full((8, 128), jnp.sum(squares) / (27 * 128 * 128), F32)
    norm_ref[...] = 1.0 / jnp.sqrt(mean + 1e-06)

    for turn in range(2):
        for index in range(8):
            halo_copy(turn, index).wait_send()

    def sent(h, d):
        ring_copy(h, d).wait_send()
        mid_copy(h, d).wait_send()
        thin_copy(h, d).wait_send()
        wide_copy(h, d).wait_send()

    each_peer(sent)
    for d in range(1, nx):
        row_copy(d).wait_send()

    def sent_to_partner(q, carry):
        for h in range(2):
            pair_copy(h, q).wait_send()
            core_copy(h, q).wait_send()
        return carry

    lax.fori_loop(0, ring, sent_to_partner, 0)


def on_device(sizes, features, occupancy, neighbors, point_voxel, conv_weight, head_weight, teacher):
    nx, ring, per, used = sizes
    rows = 64 // ring
    dma = pltpu.SemaphoreType.DMA
    vmem = pl.BlockSpec(memory_space=pltpu.VMEM)
    grad, summed, norm = pl.pallas_call(
        functools.partial(kernel, sizes),
        out_shape=(
            jax.ShapeDtypeStruct((4, 128, 128), BF16),
            jax.ShapeDtypeStruct((27, 128, 128), F32),
            jax.ShapeDtypeStruct((8, 128), F32),
        ),
        in_specs=[
            pl.BlockSpec(memory_space=pltpu.SMEM),
            vmem, vmem, vmem,
            pl.BlockSpec(memory_space=pl.ANY),
            vmem, vmem,
        ],
        out_specs=(vmem, vmem, vmem),
        scratch_shapes=[
            pltpu.VMEM((10, 10, 8, 128), F32),
            pltpu.VMEM((8, 8, 8, 128), F32),
            pltpu.VMEM((640, 1152), BF16),
            pltpu.VMEM((640, 1152), BF16),
            pltpu.VMEM((27, 128, 128), BF16),
            pltpu.VMEM((3, 128, 1152), BF16),
            pltpu.VMEM((2, 8, 64, 128), BF16),
            pltpu.VMEM((2, 8, 64, 128), BF16),
            pltpu.VMEM((2 * HALF, 128, 128), F32),
            pltpu.VMEM((2, ring, HALF * rows, 128), BF16),
            pltpu.VMEM((2, ring, HALF * rows, 128), BF16),
            pltpu.VMEM((2, ring, HALF * rows, 128), BF16),
            pltpu.VMEM((2, ring, HALF * rows, 128), BF16),
            pltpu.VMEM((2, per * ring, rows, 128), F32),
            pltpu.VMEM((2, ring, per, rows, 128), F32),
            pltpu.VMEM((2, per, rows, 128), F32),
            pltpu.VMEM((nx, 2, per, rows, 128), F32),
            pltpu.VMEM((2, per * rows, 128), BF16),
            pltpu.VMEM((2, 2, ring, ring, per * rows, 128), BF16),
            dma,
            dma((2, 8)), dma((2, 8)),
            dma((2, ring)), dma((2, ring)),
            dma((2, ring)), dma((2, ring)),
            dma((2, ring)), dma((2, ring)),
            dma((nx,)), dma((nx,)),
            dma((2, ring)), dma((2, ring)),
            dma((2, ring)), dma((2, ring)),
            dma((2, ring)), dma((2, ring)),
        ],
        compiler_params=pltpu.CompilerParams(
            collective_id=0, has_side_effects=True, vmem_limit_bytes=48 * 1024 * 1024
        ),
    )(
        neighbors, occupancy, features, point_voxel.reshape(1, -1), conv_weight,
        head_weight, teacher,
    )
    return grad, summed * norm[0, 0]


def solution(mesh):
    ring = mesh.shape["ty"] // 2
    nx = mesh.shape["tx"] // ring
    per = -(-HALF // ring)
    used = -(-HALF // per)
    in_specs = (
        P(("tx", "ty"), None, None),
        P(("tx", "ty"), None),
        P(None, ("tx", "ty")),
        P(("tx", "ty")),
        P(),
        P(),
        P(None, ("tx", "ty")),
    )
    out_specs = (P(("tx", "ty"), None, None), P())
    return jax.shard_map(
        functools.partial(on_device, (nx, ring, per, used)),
        mesh=mesh, in_specs=in_specs, out_specs=out_specs, check_vma=False,
    )
```

time: 437 us -> 68.4 us (0.16)
  waiting for transfers between devices: 233 us -> 0 us
  local copies, waits for them, and re-layouts: 91.5 us -> 6.82 us
  Pallas kernels: 0 us -> 58.5 us
  other arithmetic: 57.9 us -> 2.05 us
  starting transfers between devices: 26.9 us -> 0 us
  between operations: 17.1 us -> 0.65 us
  matrix products: 7.81 us -> 0 us
    psum x1 -> x0, waiting for transfers between devices: 231 us -> none  [normalise_terms(): summed = lax.psum(local_terms, ('tx', 'ty'))]
    pallas_call x0 -> x1, Pallas kernels: none -> 58.5 us  [on_device(): pl.pallas_call(functools.partial(kernel, sizes), out_shape=(jax.ShapeDtyp...]
    gather x57 -> x0, local copies, waits for them, and re-layouts: 51.1 us -> none  [the longest x54 45.3 us: assemble_blocks(): pieces.append(jnp.take(window, index[offset], axis=0))]
    ppermute x8 -> x0, starting transfers between devices: 26.8 us -> none  [the longest x4 17.1 us: with_halo(): lax.ppermute(tail, axis, [(i, (i + 1) % count) for i in range(ends)])]
    select_n x83 -> x0, other arithmetic: 19.4 us -> none  [the longest x81 17.6 us: assemble_blocks(): pieces.append(jnp.take(window, index[offset], axis=0))]
    slice x29 -> x1, local copies, waits for them, and re-layouts: 15.5 us -> 0.51 us  [on_device(): return (grad, summed * norm[0, 0])]
    unnamed x282 -> x14, local copies, waits for them, and re-layouts: 15.3 us -> 6.31 us
    concatenate x16 -> x0, other arithmetic: 8.49 us -> none  [the longest x3 2.73 us: with_halo(): jnp.concatenate([lax.ppermute(tail, axis, [(i, (i + 1) % count) for i in...]
  transfers between devices with their start and end apart: 9 -> 0, of which waited for: 3 -> 0; matrix products, arithmetic and copies ran while one was open for 20% -> 0% of each run, Pallas kernels for 0% -> 0%
where the time goes in v1:
time: 68.4 us; the launch traced here: 68.1 us
  Pallas kernels  58.5 us (86%)
  local copies, waits for them, and re-layouts  6.82 us (10%)
  other arithmetic  2.05 us (3%)
    pallas_call x1, Pallas kernels, on_device(): pl.pallas_call(functools.partial(kernel, sizes), out_shape=(jax.ShapeDtyp...  58.5 us
    unnamed x14, local copies, waits for them, and re-layouts  6.31 us
    mul x1, other arithmetic, on_device(): return (grad, summed * norm[0, 0])  2.05 us

profile of v1, /device:TPU:1, one launch (start us, length us, event | category | flops | bytes accessed | tf_op | source)
XLA Modules:
  0.0 68.1 jit_solution(15373618536158353319)
XLA Ops:
  0.6 0.8 %copy.9.near_ref = s32[27,4]{1,0:T(8,128)S(1)} copy(s32[27,4]{0,1:T(4,128)} %param.9) | data formatting | bytes 864 | tf_op args[2]
  1.4 0.0 copy-start
  1.4 1.2 %copy-done = bf16[27,128,128]{2,1,0:T(8,128)(2,1)S(1)} copy-done((bf16[27,128,128]{2,1,0:T(8,128)(2,1)S(1)}, bf16[27,128,128]{2,1,0:T(8,128)(2,1)}, u32[]{:S(2)}) %copy-start) | copy-done | bytes 884760
  2.6 0.0 copy-start.1
  2.6 0.9 %copy-done.1 = bf16[4,128,128]{2,1,0:T(8,128)(2,1)S(1)} copy-done((bf16[4,128,128]{2,1,0:T(8,128)(2,1)S(1)}, bf16[4,128,128]{2,1,0:T(8,128)(2,1)}, u32[]{:S(2)}) %copy-start.1) | copy-done | bytes 131096
  3.5 0.0 copy-start.2
  3.5 0.8 %copy-done.2 = bf16[16,1024]{1,0:T(8,128)(2,1)S(1)} copy-done((bf16[16,1024]{1,0:T(8,128)(2,1)S(1)}, bf16[16,1024]{1,0:T(8,128)(2,1)}, u32[]{:S(2)}) %copy-start.2) | copy-done | bytes 32792
  4.2 0.0 copy-start.3
  4.2 0.7 %copy-done.3 = s32[1024]{0:T(1024)S(1)} copy-done((s32[1024]{0:T(1024)S(1)}, s32[1024]{0:T(1024)}, u32[]{:S(2)}) %copy-start.3) | copy-done | bytes 4120
  4.9 0.0 copy-start.4
  4.9 0.7 %copy-done.4 = bf16[16,128]{1,0:T(8,128)(2,1)S(1)} copy-done((bf16[16,128]{1,0:T(8,128)(2,1)S(1)}, bf16[16,128]{1,0:T(8,128)(2,1)}, u32[]{:S(2)}) %copy-start.4) | copy-done | bytes 4120
  5.6 0.0 copy-start.5
  5.6 0.7 copy-done.5
  6.3 58.5 %shard_map.86 = (bf16[4,128,128]{2,1,0:T(8,128)(2,1)S(1)}, f32[27,128,128]{2,1,0:T(8,128)S(1)}, f32[8,128]{1,0:T(8,128)S(1)}) custom-call(s32[27,4]{1,0:T(8,128)S(1)} %copy.9.near_ref, s32[4,128]{1,0:T(4,128)S(1)} %copy-done.5, bf16[4,128,128]{2,1,0:T(8,128)(2,1)S(1)} %copy-done.1, s32[1,1024]{1,0:T(1,128)S(1)} %bitcast.2, ...), custom_call_target="tpu_custom_call" | custom-call | tf_op jit(solution)/shard_map/pallas_call | solution.py:403
  64.8 0.5 slice.3
  65.4 2.0 %broadcast_multiply_fusion = f32[27,128,128]{2,1,0:T(8,128)} fusion(f32[27,128,128]{2,1,0:T(8,128)S(1)} %get-tuple-element.6, f32[]{:T(128)} %bitcast.1), kind=kLoop, calls=%fused_computation | loop fusion | flops 442368 | bytes 3538948 | tf_op jit(solution)/shard_map/mul | solution.py:454
  67.4 0.7 copy.11
Async XLA Ops:
  1.4 1.2 %copy-start = (bf16[27,128,128]{2,1,0:T(8,128)(2,1)S(1)}, bf16[27,128,128]{2,1,0:T(8,128)(2,1)}, u32[]{:S(2)}) copy-start(bf16[27,128,128]{2,1,0:T(8,128)(2,1)} %weight_hbm.1) | copy-start | bytes 2654212
  2.6 0.9 %copy-start.1 = (bf16[4,128,128]{2,1,0:T(8,128)(2,1)S(1)}, bf16[4,128,128]{2,1,0:T(8,128)(2,1)}, u32[]{:S(2)}) copy-start(bf16[4,128,128]{2,1,0:T(8,128)(2,1)} %feat_ref.1) | copy-start | bytes 393220
  3.5 0.8 %copy-start.2 = (bf16[16,1024]{1,0:T(8,128)(2,1)S(1)}, bf16[16,1024]{1,0:T(8,128)(2,1)}, u32[]{:S(2)}) copy-start(bf16[16,1024]{1,0:T(8,128)(2,1)} %teacher_ref.1) | copy-start | bytes 98308
  4.2 0.7 %copy-start.3 = (s32[1024]{0:T(1024)S(1)}, s32[1024]{0:T(1024)}, u32[]{:S(2)}) copy-start(s32[1024]{0:T(1024)} %param.10) | copy-start | bytes 12292
  4.9 0.7 %copy-start.4 = (bf16[16,128]{1,0:T(8,128)(2,1)S(1)}, bf16[16,128]{1,0:T(8,128)(2,1)}, u32[]{:S(2)}) copy-start(bf16[16,128]{1,0:T(8,128)(2,1)} %head_ref.1) | copy-start | bytes 12292
  5.6 0.7 %copy-start.5 = (s32[4,128]{1,0:T(4,128)S(1)}, s32[4,128]{1,0:T(4,128)}, u32[]{:S(2)}) copy-start(s32[4,128]{1,0:T(4,128)} %occ_ref.1) | copy-start | bytes 6148

commit v2 on v1

v2 whole, which is shorter than its diff:
```python
import functools

import jax
import jax.numpy as jnp
from jax import lax
from jax.experimental import pallas as pl
from jax.experimental.pallas import tpu as pltpu
from jax.sharding import PartitionSpec as P

F32 = jnp.float32
BF16 = jnp.bfloat16
MESH = pl.DeviceIdType.MESH
ROUTES = ((-1, 0), (1, 0), (0, -1), (0, 1), (-1, -1), (-1, 1), (1, -1), (1, 1))
TN = (((0,), (0,)), ((), ()))
NT = (((1,), (1,)), ((), ()))
PARTS = ((0, 8, "yzx"), (8, 8, "zyx"), (16, 11, "xyz"))


def far_first(n):
    return sorted(range(1, n), key=lambda d: (-min(d, n - d), d))


def near_first(n):
    return sorted(range(n), key=lambda d: (min(d, n - d), d))


def slot_groups(n):
    if n < 4:
        return [(s, s + 1) for s in range(n)]
    return [(0, 3), (3, n - 1), (n - 1, n)]


class Part:
    def __init__(self, place, first, count, axes, size):
        self.index = place
        self.first, self.count = first, count
        self.a1, self.a2, self.a3 = axes
        self.n1, self.n2, self.n3 = (size[axis] for axis in axes)
        self.rows = 64 // self.n1
        self.tiles = count * self.rows // 8
        self.per = -(-self.tiles // self.n2)
        self.near2 = near_first(self.n2)
        self.groups = slot_groups(self.n2)


def make_parts(nx, ring):
    size = {"x": nx, "y": ring, "z": ring}
    return [Part(i, *spec, size) for i, spec in enumerate(PARTS)]


def scratch_of(part):
    dma = pltpu.SemaphoreType.DMA
    wide = pltpu.VMEM((part.n1, part.tiles * 8, 128), BF16)
    return {
        "pair_out": wide, "pair_in": wide, "ring_out": wide, "ring_in": wide,
        "mid": pltpu.VMEM((part.n2 * part.per, 8, 128), F32),
        "mid_in": pltpu.VMEM((part.n2, part.per, 8, 128), F32),
        "row_out": pltpu.VMEM((part.per, 8, 128), F32),
        "row_in": pltpu.VMEM((part.n3, part.per, 8, 128), F32),
        "full": pltpu.VMEM((2, part.n1, part.n2, part.per * 8, 128), BF16),
        "tiles": pltpu.VMEM((part.n2 * part.per, 8, 128), F32),
        "pair_send": dma((part.n1,)), "pair_recv": dma((part.n1,)),
        "ring_send": dma((part.n1,)), "ring_recv": dma((part.n1,)),
        "mid_send": dma((part.n2,)), "mid_recv": dma((part.n2,)),
        "row_send": dma((part.n3,)), "row_recv": dma((part.n3,)),
        "thin_send": dma((part.n2,)), "thin_recv": dma((part.n2,)),
        "wide_send": dma((len(part.groups), part.n1)),
        "wide_recv": dma((len(part.groups), part.n1)),
        "core_send": dma((len(part.groups), part.n1)),
        "core_recv": dma((len(part.groups), part.n1)),
    }


def span_to_send(step):
    if step < 0:
        return slice(1, 2)
    if step > 0:
        return slice(8, 9)
    return slice(1, 9)


def span_received(step):
    if step < 0:
        return slice(9, 10)
    if step > 0:
        return slice(0, 1)
    return slice(1, 9)


def split3(value):
    one = value.astype(BF16)
    rest = value - one.astype(F32)
    two = rest.astype(BF16)
    three = (rest - two.astype(F32)).astype(BF16)
    return one, two, three


def kernel(sizes, names, *refs):
    nx, ring = sizes
    parts = make_parts(nx, ring)
    in_hbm, (grad_ref, sum_ref, norm_ref) = refs[:7], refs[7:10]
    (
        near_ref, occ_ref, feat_ref, point_ref, weight, head_ref, teacher_ref, input_sem,
        cells, occ_cells, columns, columns_g, weight_t, halo_out, halo_in, terms,
        halo_send, halo_recv,
    ) = refs[10:28]
    rest = iter(refs[28:])
    for part in parts:
        for name in names:
            setattr(part, name, next(rest))

    n_tx, n_ty = nx * ring, 2 * ring
    tx = lax.axis_index("tx")
    ty = lax.axis_index("ty")
    core = ty % 2
    place = {"x": tx // ring, "z": tx % ring, "y": ty // 2}
    extent = {"x": nx, "y": ring, "z": ring}

    def along(axis, d):
        if axis == "x":
            return (((place["x"] + d) % nx) * ring + place["z"], ty)
        if axis == "z":
            return (place["x"] * ring + (place["z"] + d) % ring, ty)
        return (tx, ((place["y"] + d) % ring) * 2 + core)

    peers = {axis: [along(axis, d) for d in range(extent[axis])] for axis in "xyz"}
    partner = (tx, place["y"] * 2 + 1 - core)

    def toward(route):
        ex, ey = route
        return ((tx + ex + n_tx) % n_tx, (ty + ey + n_ty) % n_ty)

    def remote(src, dst, send, recv, device):
        return pltpu.make_async_remote_copy(
            src_ref=src, dst_ref=dst, send_sem=send, recv_sem=recv,
            device_id=device, device_id_type=MESH,
        )

    barrier = pltpu.get_barrier_semaphore()

    def greet(device):
        pl.semaphore_signal(barrier, inc=1, device_id=device, device_id_type=MESH)

    for route in ROUTES:
        greet(toward(route))
    held = (near_ref, occ_ref, feat_ref, point_ref, weight, head_ref, teacher_ref)
    inputs = [
        pltpu.make_async_copy(src, dst, input_sem.at[i])
        for i, (src, dst) in enumerate(zip(in_hbm, held))
    ]
    for i in (0, 1, 2, 3, 6, 5, 4):
        inputs[i].start()
    greet(partner)
    for axis in "yzx":
        for d in far_first(extent[axis]):
            greet(peers[axis][d])

    for i in (0, 1, 2):
        inputs[i].wait()
    active = (near_ref[:, 13:14] >= 0).astype(jnp.int32)
    occupancy = (occ_ref[...] * active).astype(F32)
    for slot in range(4):
        i, j = slot // 2, slot % 2
        column = jnp.broadcast_to(occupancy[slot : slot + 1, :], (128, 128)).T
        occ_cells[4 * i : 4 * i + 4, 4 * j : 4 * j + 4] = column.reshape(4, 4, 8, 128)
        masked = feat_ref[slot].astype(F32) * column
        cells[1 + 4 * i : 5 + 4 * i, 1 + 4 * j : 5 + 4 * j] = masked.reshape(4, 4, 8, 128)

    def halo_copy(turn, index):
        count = 64 if index < 4 else 16
        return remote(
            halo_out.at[turn, index, 0:count], halo_in.at[turn, index, 0:count],
            halo_send.at[turn, index], halo_recv.at[turn, index], toward(ROUTES[index]),
        )

    def stage_halo(turn):
        for index, (ex, ey) in enumerate(ROUTES):
            block = cells[span_to_send(ex), span_to_send(ey)]
            if index < 4:
                halo_out[turn, index] = block.reshape(64, 128).astype(BF16)
            else:
                block = block.reshape(8, 128)
                halo_out[turn, index, 0:16] = jnp.concatenate([block, block], axis=0).astype(BF16)

    def send_halo(turn):
        for index in (4, 5, 6, 7, 0, 1, 2, 3):
            halo_copy(turn, index).start()

    def take_halo(turn):
        for index, (ex, ey) in enumerate(ROUTES):
            halo_copy(turn, index).wait_recv()
            from_x, from_y = tx - ex, ty - ey
            inside = (from_x >= 0) & (from_x < n_tx) & (from_y >= 0) & (from_y < n_ty)
            keep = inside.astype(jnp.int32).astype(F32)
            if index < 4:
                block = halo_in[turn, index].astype(F32) * keep
                shape = (1, 8, 8, 128) if ex else (8, 1, 8, 128)
            else:
                block = halo_in[turn, index, 0:16].astype(F32)[0:8] * keep
                shape = (1, 1, 8, 128)
            cells[span_received(ex), span_received(ey)] = block.reshape(shape)

    layer = lax.broadcasted_iota(jnp.int32, (80, 8, 128), 1)

    def fill_columns(target, flip):
        for dy in range(3):
            start = 2 - dy if flip else dy
            block = cells[:, start : start + 8].reshape(80, 8, 128)
            for dz in range(3):
                move = 1 - dz if flip else dz - 1
                if move > 0:
                    shifted = jnp.where(layer == 7, 0.0, pltpu.roll(block, 7, 1))
                elif move < 0:
                    shifted = jnp.where(layer == 0, 0.0, pltpu.roll(block, 1, 1))
                else:
                    shifted = block
                lane = 128 * (3 * dy + dz)
                target[:, lane : lane + 128] = shifted.reshape(640, 128).astype(BF16)

    stage_halo(0)
    pl.semaphore_wait(barrier, 9 + 2 * (ring - 1) + nx - 1)
    send_halo(0)

    for i in (3, 6, 5, 4):
        inputs[i].wait()
    teacher = jnp.exp(teacher_ref[...].astype(F32))
    target = teacher / jnp.sum(teacher, axis=0, keepdims=True)
    where = point_ref[...]
    spread = (
        (where // 256) * 256 + (where // 32) % 4 * 64
        + (where // 128) % 2 * 32 + where % 32
    )
    voxel = lax.broadcasted_iota(jnp.int32, (512, 1024), 0)
    hits = jnp.where(voxel == spread, 1.0, 0.0).astype(BF16)
    stack = jnp.concatenate([*split3(target), jnp.ones((16, 1024), BF16)], axis=0)
    sums = lax.dot_general(stack, hits, NT, preferred_element_type=F32)
    target_sum = sums[0:16] + (sums[16:32] + sums[32:48])
    points = sums[48:64]

    for k in range(27):
        lane = 128 * (k % 9)
        weight_t[k // 9, :, lane : lane + 128] = weight[k]

    take_halo(0)
    fill_columns(columns, False)

    pre = jnp.zeros((512, 128), F32)
    for q in range(3):
        pre += jnp.dot(
            columns[64 * q : 64 * q + 512, :],
            weight[9 * q : 9 * q + 9].reshape(1152, 128),
            preferred_element_type=F32,
        )
    occupied = occ_cells[...].reshape(512, 128)
    logistic = 1.0 / (1.0 + jnp.exp(-pre))
    hidden = (pre * logistic * occupied).astype(BF16)
    slope = logistic * (1.0 + pre * (1.0 - logistic)) * occupied

    logits = lax.dot_general(head_ref[...], hidden, NT, preferred_element_type=F32)
    student = jnp.exp(logits)
    student = student / jnp.sum(student, axis=0, keepdims=True)
    slope_logits = jnp.where(points > 0.0, points * student - target_sum, 0.0)
    head3 = jnp.concatenate([head_ref[...]] * 3, axis=0)
    pieces = jnp.concatenate(split3(slope_logits), axis=0)
    dhidden = lax.dot_general(pieces, head3, TN, preferred_element_type=F32)
    dpre = (dhidden * slope).astype(BF16)

    cells[1:9, 1:9] = dpre.astype(F32).reshape(8, 8, 8, 128)
    stage_halo(1)
    send_halo(1)

    def own_rows(part, side, q):
        return pl.ds(pl.multiple_of(side * 64 + q * part.rows, part.rows), part.rows)

    def pair_copy(part, q):
        return remote(
            part.pair_out.at[q], part.pair_in.at[q],
            part.pair_send.at[q], part.pair_recv.at[q], partner,
        )

    def block_at(part, d):
        return (place[part.a1] + d) % part.n1

    def my_term(part, side, q):
        block = terms[part.first : part.first + part.count, own_rows(part, side, q), :]
        return block.reshape(part.tiles * 8, 128)

    for turn, part in enumerate(parts):
        term = lax.dot_general(
            columns[64 * turn : 64 * turn + 512, :], dpre, TN, preferred_element_type=F32
        )
        terms[9 * turn : 9 * turn + 9] = term.reshape(9, 128, 128)
        for d in far_first(part.n1) + [0]:
            q = block_at(part, d)
            part.pair_out[q] = my_term(part, 1 - core, q).astype(BF16)
            pair_copy(part, q).start()

    def ring_copy(part, d):
        return remote(
            part.ring_out.at[d], part.ring_in.at[d],
            part.ring_send.at[d], part.ring_recv.at[d], peers[part.a1][d],
        )

    def paired(part, q):
        pair_copy(part, q).wait_recv()
        return my_term(part, core, q) + part.pair_in[q].astype(F32)

    orders = {part.index: far_first(part.n1) for part in parts}
    for turn in range(max(len(order) for order in orders.values())):
        for part in parts:
            if turn < len(orders[part.index]):
                d = orders[part.index][turn]
                part.ring_out[d] = paired(part, block_at(part, d)).astype(BF16)
                ring_copy(part, d).start()
    for part in parts:
        own = paired(part, block_at(part, 0))
        part.mid[0 : part.tiles] = own.reshape(part.tiles, 8, 128)
        spare = part.per * part.n2 - part.tiles
        if spare:
            part.mid[part.tiles :] = jnp.zeros((spare, 8, 128), F32)

    take_halo(1)
    fill_columns(columns_g, True)
    back = jnp.zeros((512, 128), F32)
    for q in range(3):
        back += lax.dot_general(
            columns_g[64 * (2 - q) : 64 * (2 - q) + 512, :], weight_t[q], NT,
            preferred_element_type=F32,
        )
    back = (back * occ_cells[...].reshape(512, 128)).reshape(8, 8, 8, 128)
    for slot in range(4):
        i, j = slot // 2, slot % 2
        block = back[4 * i : 4 * i + 4, 4 * j : 4 * j + 4]
        grad_ref[slot] = block.reshape(128, 128).astype(BF16)

    def mid_copy(part, d):
        p = (place[part.a2] + d) % part.n2
        return remote(
            part.mid.at[pl.ds(p * part.per, part.per)], part.mid_in.at[d],
            part.mid_send.at[d], part.mid_recv.at[d], peers[part.a2][d],
        )

    last_first = (parts[2], parts[0], parts[1])
    for part in last_first:
        block = part.mid[0 : part.tiles]
        for d in reversed(far_first(part.n1)):
            ring_copy(part, d).wait_recv()
            block = block + part.ring_in[d].astype(F32).reshape(part.tiles, 8, 128)
        part.mid[0 : part.tiles] = block
        for d in far_first(part.n2):
            mid_copy(part, d).start()

    def row_copy(part, d):
        return remote(
            part.row_out, part.row_in.at[place[part.a3]],
            part.row_send.at[d], part.row_recv.at[d], peers[part.a3][d],
        )

    for part in last_first:
        block = part.mid[pl.ds(place[part.a2] * part.per, part.per)]
        for d in reversed(far_first(part.n2)):
            mid_copy(part, d).wait_recv()
            block = block + part.mid_in[d]
        part.row_out[...] = block
        for d in far_first(part.n3):
            row_copy(part, d).start()
        part.row_in[place[part.a3]] = block

    def thin_copy(part, slot):
        home = part.full.at[core, place[part.a1]]
        return remote(
            home.at[0], home.at[slot],
            part.thin_send.at[slot], part.thin_recv.at[slot],
            peers[part.a2][part.near2[slot]],
        )

    def wide_copy(part, group, d):
        start, stop = part.groups[group]
        block = part.full.at[core, place[part.a1], start:stop]
        return remote(
            block, block, part.wide_send.at[group, d], part.wide_recv.at[group, d],
            peers[part.a1][d],
        )

    def core_copy(part, group, q):
        start, stop = part.groups[group]
        block = part.full.at[core, q, start:stop]
        return remote(
            block, block, part.core_send.at[group, q], part.core_recv.at[group, q], partner
        )

    for part in (parts[0], parts[1], parts[2]):
        for d in reversed(far_first(part.n3)):
            row_copy(part, d).wait_recv()
        total = part.row_in[0]
        for x in range(1, part.n3):
            total = total + part.row_in[x]
        part.full[core, place[part.a1], 0] = total.reshape(part.per * 8, 128).astype(BF16)
        for slot in reversed(range(1, part.n2)):
            thin_copy(part, slot).start()

    rounds = max(len(part.groups) for part in parts)
    for group in range(rounds):
        for part in parts:
            start, stop = part.groups[group]
            for slot in range(max(start, 1), stop):
                thin_copy(part, slot).wait_recv()
            for d in far_first(part.n1):
                wide_copy(part, group, d).start()
            core_copy(part, group, block_at(part, 0)).start()
    for group in range(rounds):
        for part in parts:
            for d in reversed(far_first(part.n1)):
                wide_copy(part, group, d).wait_recv()
                core_copy(part, group, block_at(part, part.n1 - d)).start()

    squares = jnp.zeros((8, 128), F32)
    for part in parts:
        where = [
            (place[part.a2] + part.n2 - part.near2[slot]) % part.n2 for slot in range(part.n2)
        ]
        for step in range(2 * part.n1):
            side, q = step // part.n1, step % part.n1
            if side == 0:
                side = core
            else:
                side = 1 - core
                for group in range(len(part.groups)):
                    core_copy(part, group, q).wait_recv()
            for slot in range(part.n2):
                piece = part.full[side, q, slot].astype(F32).reshape(part.per, 8, 128)
                part.tiles_ref[pl.ds(where[slot] * part.per, part.per)] = piece
            block = part.tiles_ref[0 : part.tiles]
            squares = squares + jnp.sum(block * block, axis=0)
            sum_ref[part.first : part.first + part.count, own_rows(part, side, q), :] = (
                block.reshape(part.count, part.rows, 128)
            )
    mean = jnp.full((8, 128), jnp.sum(squares) / (27 * 128 * 128), F32)
    norm_ref[...] = 1.0 / jnp.sqrt(mean + 1e-06)

    for turn in range(2):
        for index in range(8):
            halo_copy(turn, index).wait_send()
    for part in parts:
        for q in range(part.n1):
            pair_copy(part, q).wait_send()
            for group in range(len(part.groups)):
                core_copy(part, group, q).wait_send()
        for d in range(1, part.n1):
            ring_copy(part, d).wait_send()
            for group in range(len(part.groups)):
                wide_copy(part, group, d).wait_send()
        for d in range(1, part.n2):
            mid_copy(part, d).wait_send()
            thin_copy(part, d).wait_send()
        for d in range(1, part.n3):
            row_copy(part, d).wait_send()


def finish_kernel(grad_ref, sum_ref, norm_ref, grad_out, sum_out, staged, sems):
    grad_copy = pltpu.make_async_copy(grad_ref, grad_out, sems.at[9])
    grad_copy.start()
    norm = norm_ref[...].reshape(1, 1, 8, 128)
    copies = []
    for step in range(9):
        span = slice(3 * step, 3 * step + 3)
        block = sum_ref[span].reshape(3, 16, 8, 128) * norm
        staged[span] = block.reshape(3, 128, 128)
        copies.append(pltpu.make_async_copy(staged.at[span], sum_out.at[span], sems.at[step]))
        copies[-1].start()
    for copy in copies:
        copy.wait()
    grad_copy.wait()


def on_device(sizes, features, occupancy, neighbors, point_voxel, conv_weight, head_weight, teacher):
    nx, ring = sizes
    parts = make_parts(nx, ring)
    dma = pltpu.SemaphoreType.DMA
    vmem = pl.BlockSpec(memory_space=pltpu.VMEM)
    hbm = pl.BlockSpec(memory_space=pltpu.HBM)
    args = (
        neighbors.T, occupancy, features, point_voxel.reshape(1, -1), conv_weight,
        head_weight, teacher,
    )
    own = [scratch_of(part) for part in parts]
    names = ["tiles_ref" if name == "tiles" else name for name in own[0]]
    grad, summed, norm = pl.pallas_call(
        functools.partial(kernel, sizes, names),
        out_shape=(
            jax.ShapeDtypeStruct((4, 128, 128), BF16),
            jax.ShapeDtypeStruct((27, 128, 128), F32),
            jax.ShapeDtypeStruct((8, 128), F32),
        ),
        in_specs=[hbm] * 7,
        out_specs=(vmem, vmem, vmem),
        scratch_shapes=[
            *(pltpu.VMEM(arg.shape, arg.dtype) for arg in args),
            dma((7,)),
            pltpu.VMEM((10, 10, 8, 128), F32),
            pltpu.VMEM((8, 8, 8, 128), F32),
            pltpu.VMEM((640, 1152), BF16),
            pltpu.VMEM((640, 1152), BF16),
            pltpu.VMEM((3, 128, 1152), BF16),
            pltpu.VMEM((2, 8, 64, 128), BF16),
            pltpu.VMEM((2, 8, 64, 128), BF16),
            pltpu.VMEM((27, 128, 128), F32),
            dma((2, 8)), dma((2, 8)),
            *(shape for table in own for shape in table.values()),
        ],
        compiler_params=pltpu.CompilerParams(
            collective_id=0, has_side_effects=True, vmem_limit_bytes=48 * 1024 * 1024
        ),
    )(*(pltpu.with_memory_space_constraint(arg, pltpu.HBM) for arg in args))
    return pl.pallas_call(
        finish_kernel,
        out_shape=(
            jax.ShapeDtypeStruct((4, 128, 128), BF16),
            jax.ShapeDtypeStruct((27, 128, 128), F32),
        ),
        in_specs=[vmem, vmem, vmem],
        out_specs=(hbm, hbm),
        scratch_shapes=[pltpu.VMEM((27, 128, 128), F32), dma((10,))],
        compiler_params=pltpu.CompilerParams(vmem_limit_bytes=16 * 1024 * 1024),
    )(grad, summed, norm)


def solution(mesh):
    ring = mesh.shape["ty"] // 2
    nx = mesh.shape["tx"] // ring
    in_specs = (
        P(("tx", "ty"), None, None),
        P(("tx", "ty"), None),
        P(None, ("tx", "ty")),
        P(("tx", "ty")),
        P(),
        P(),
        P(None, ("tx", "ty")),
    )
    out_specs = (P(("tx", "ty"), None, None), P())
    return jax.shard_map(
        functools.partial(on_device, (nx, ring)),
        mesh=mesh, in_specs=in_specs, out_specs=out_specs, check_vma=False,
    )
```

time: 68.4 us -> 56.9 us (0.83)
  local copies, waits for them, and re-layouts: 6.82 us -> 0 us
  Pallas kernels: 58.5 us -> 56.1 us
  other arithmetic: 2.05 us -> 0 us
    unnamed x14 -> x0, local copies, waits for them, and re-layouts: 6.31 us -> none
    pallas_call x1 -> x2, Pallas kernels: 58.5 us -> 56.1 us  [the longest x1 54.8 us: on_device(): pl.pallas_call(functools.partial(kernel, sizes, names), out_shape=(jax.Sh...]
    mul x1 -> x0, other arithmetic: 2.05 us -> none  [on_device(): return (grad, summed * norm[0, 0])]
where the time goes in v2:
time: 56.9 us; the launch traced here: 56.8 us
  Pallas kernels  56.1 us (99%)
  between operations  0.64 us (1%)
    pallas_call x1, Pallas kernels, on_device(): pl.pallas_call(functools.partial(kernel, sizes, names), out_shape=(jax.Sh...  54.8 us
    pallas_call x1, Pallas kernels, on_device(): pl.pallas_call(finish_kernel, out_shape=(jax.ShapeDtypeStruct((4, 128, 12...  1.33 us

profile of v2, /device:TPU:1, one launch (start us, length us, event | category | flops | bytes accessed | tf_op | source)
XLA Modules:
  0.0 56.8 jit_solution(17946746649577953099)
XLA Ops:
  0.6 54.8 %shard_map.86 = (bf16[4,128,128]{2,1,0:T(8,128)(2,1)S(1)}, f32[27,128,128]{2,1,0:T(8,128)S(1)}, f32[8,128]{1,0:T(8,128)S(1)}) custom-call(s32[4,27]{1,0:T(4,128)} %bitcast.3, s32[4,128]{1,0:T(4,128)} %refs_1_.1, bf16[4,128,128]{2,1,0:T(8,128)(2,1)} %refs_2_.1, s32[1,1024]{1,0:T(1,128)} %bitcast.2, bf16[27,128,128]{2,1,0:T(8,128)(2,1)} %refs_4_.1, ...), custom_call_target="tpu_custom_call" | custom-call | tf_op jit(solution)/shard_map/pallas_call | solution.py:488
  55.5 1.3 %shard_map.87 = (bf16[4,128,128]{2,1,0:T(8,128)(2,1)}, f32[27,128,128]{2,1,0:T(8,128)}) custom-call(bf16[4,128,128]{2,1,0:T(8,128)(2,1)S(1)} %get-tuple-element.5.grad_ref, f32[27,128,128]{2,1,0:T(8,128)S(1)} %get-tuple-element.6.sum_ref, f32[8,128]{1,0:T(8,128)S(1)} %get-tuple-element.7.norm_ref), custom_call_target="tpu_custom_call" | custom-call | tf_op jit(solution)/shard_map/pallas_call | solution.py:515

commit v3 on v2

--- a/solution.py
+++ b/solution.py
@@ -24,10 +24,9 @@
     return sorted(range(n), key=lambda d: (min(d, n - d), d))
 
 
-def slot_groups(n):
-    if n < 4:
-        return [(s, s + 1) for s in range(n)]
-    return [(0, 3), (3, n - 1), (n - 1, n)]
+def runs(n, *cuts):
+    edges = sorted({0, n, *(cut for cut in cuts if cut < n)})
+    return list(zip(edges, edges[1:]))
 
 
 class Part:
@@ -39,8 +38,11 @@
         self.rows = 64 // self.n1
         self.tiles = count * self.rows // 8
         self.per = -(-self.tiles // self.n2)
+        self.far1 = far_first(self.n1) + [0]
+        self.near1 = near_first(self.n1)
         self.near2 = near_first(self.n2)
-        self.groups = slot_groups(self.n2)
+        self.pair_runs = runs(self.n1)
+        self.core_runs = runs(self.n1)
 
 
 def make_parts(nx, ring):
@@ -55,19 +57,18 @@
         "pair_out": wide, "pair_in": wide, "ring_out": wide, "ring_in": wide,
         "mid": pltpu.VMEM((part.n2 * part.per, 8, 128), F32),
         "mid_in": pltpu.VMEM((part.n2, part.per, 8, 128), F32),
-        "row_out": pltpu.VMEM((part.per, 8, 128), F32),
-        "row_in": pltpu.VMEM((part.n3, part.per, 8, 128), F32),
+        "row_out": pltpu.VMEM((part.per * 8, 128), F32),
+        "row_in": pltpu.VMEM((part.n3, part.per * 8, 128), F32),
         "full": pltpu.VMEM((2, part.n1, part.n2, part.per * 8, 128), BF16),
         "tiles": pltpu.VMEM((part.n2 * part.per, 8, 128), F32),
-        "pair_send": dma((part.n1,)), "pair_recv": dma((part.n1,)),
+        "squares": pltpu.VMEM((2, part.n1, 8, 128), F32),
+        "pair_send": dma((len(part.pair_runs),)), "pair_recv": dma((len(part.pair_runs),)),
         "ring_send": dma((part.n1,)), "ring_recv": dma((part.n1,)),
         "mid_send": dma((part.n2,)), "mid_recv": dma((part.n2,)),
         "row_send": dma((part.n3,)), "row_recv": dma((part.n3,)),
         "thin_send": dma((part.n2,)), "thin_recv": dma((part.n2,)),
-        "wide_send": dma((len(part.groups), part.n1)),
-        "wide_recv": dma((len(part.groups), part.n1)),
-        "core_send": dma((len(part.groups), part.n1)),
-        "core_recv": dma((len(part.groups), part.n1)),
+        "wide_send": dma((part.n1,)), "wide_recv": dma((part.n1,)),
+        "core_send": dma((len(part.core_runs),)), "core_recv": dma((len(part.core_runs),)),
     }
 
 
@@ -102,9 +103,9 @@
     (
         near_ref, occ_ref, feat_ref, point_ref, weight, head_ref, teacher_ref, input_sem,
         cells, occ_cells, columns, columns_g, weight_t, halo_out, halo_in, terms,
-        halo_send, halo_recv,
-    ) = refs[10:28]
-    rest = iter(refs[28:])
+        halo_send, halo_recv, word_sem,
+    ) = refs[10:29]
+    rest = iter(refs[29:])
     for part in parts:
         for name in names:
             setattr(part, name, next(rest))
@@ -141,8 +142,15 @@
     def greet(device):
         pl.semaphore_signal(barrier, inc=1, device_id=device, device_id_type=MESH)
 
-    for route in ROUTES:
-        greet(toward(route))
+    def on_map(x, y):
+        return (x >= 0) & (x < n_tx) & (y >= 0) & (y < n_ty)
+
+    leads = [on_map(tx + ex, ty + ey) for ex, ey in ROUTES]
+    comes = [on_map(tx - ex, ty - ey) for ex, ey in ROUTES]
+    greeted = 0
+    for route, valid in zip(ROUTES, leads):
+        pl.when(valid)(functools.partial(greet, toward(route)))
+        greeted = greeted + valid.astype(jnp.int32)
     held = (near_ref, occ_ref, feat_ref, point_ref, weight, head_ref, teacher_ref)
     inputs = [
         pltpu.make_async_copy(src, dst, input_sem.at[i])
@@ -150,10 +158,23 @@
     ]
     for i in (0, 1, 2, 3, 6, 5, 4):
         inputs[i].start()
-    greet(partner)
-    for axis in "yzx":
-        for d in far_first(extent[axis]):
-            greet(peers[axis][d])
+    others = [peers[axis][d] for axis in "yz" for d in (1, ring - 1)]
+    others += [partner] + [peers["x"][d] for d in far_first(nx)]
+    for device in others:
+        greet(device)
+
+    def pass_word(steps):
+        for i, axis in enumerate("yz"):
+            for way, d in enumerate((1, ring - 1)):
+                pl.semaphore_signal(
+                    word_sem.at[i, way, steps], inc=1, device_id=peers[axis][d],
+                    device_id_type=MESH,
+                )
+
+    def await_word(steps):
+        for i in range(2):
+            for way in range(2):
+                pl.semaphore_wait(word_sem.at[i, way, steps], 1)
 
     for i in (0, 1, 2):
         inputs[i].wait()
@@ -184,20 +205,18 @@
 
     def send_halo(turn):
         for index in (4, 5, 6, 7, 0, 1, 2, 3):
-            halo_copy(turn, index).start()
+            pl.when(leads[index])(halo_copy(turn, index).start)
 
     def take_halo(turn):
         for index, (ex, ey) in enumerate(ROUTES):
-            halo_copy(turn, index).wait_recv()
-            from_x, from_y = tx - ex, ty - ey
-            inside = (from_x >= 0) & (from_x < n_tx) & (from_y >= 0) & (from_y < n_ty)
-            keep = inside.astype(jnp.int32).astype(F32)
+            pl.when(comes[index])(halo_copy(turn, index).wait_recv)
             if index < 4:
-                block = halo_in[turn, index].astype(F32) * keep
+                block = halo_in[turn, index].astype(F32)
                 shape = (1, 8, 8, 128) if ex else (8, 1, 8, 128)
             else:
-                block = halo_in[turn, index, 0:16].astype(F32)[0:8] * keep
+                block = halo_in[turn, index, 0:16].astype(F32)[0:8]
                 shape = (1, 1, 8, 128)
+            block = jnp.where(comes[index], block, 0.0)
             cells[span_received(ex), span_received(ey)] = block.reshape(shape)
 
     layer = lax.broadcasted_iota(jnp.int32, (80, 8, 128), 1)
@@ -218,8 +237,11 @@
                 target[:, lane : lane + 128] = shifted.reshape(640, 128).astype(BF16)
 
     stage_halo(0)
-    pl.semaphore_wait(barrier, 9 + 2 * (ring - 1) + nx - 1)
+    pl.semaphore_wait(barrier, greeted + len(others))
     send_halo(0)
+    farthest = ring // 2
+    if farthest >= 2:
+        pass_word(2)
 
     for i in (3, 6, 5, 4):
         inputs[i].wait()
@@ -237,6 +259,10 @@
     target_sum = sums[0:16] + (sums[16:32] + sums[32:48])
     points = sums[48:64]
 
+    for steps in range(2, farthest):
+        await_word(steps)
+        pass_word(steps + 1)
+
     for k in range(27):
         lane = 128 * (k % 9)
         weight_t[k // 9, :, lane : lane + 128] = weight[k]
@@ -272,10 +298,11 @@
     def own_rows(part, side, q):
         return pl.ds(pl.multiple_of(side * 64 + q * part.rows, part.rows), part.rows)
 
-    def pair_copy(part, q):
-        return remote(
-            part.pair_out.at[q], part.pair_in.at[q],
-            part.pair_send.at[q], part.pair_recv.at[q], partner,
+    def pair_copy(part, run):
+        start, stop = part.pair_runs[run]
+        return remote(
+            part.pair_out.at[start:stop], part.pair_in.at[start:stop],
+            part.pair_send.at[run], part.pair_recv.at[run], partner,
         )
 
     def block_at(part, d):
@@ -285,15 +312,16 @@
         block = terms[part.first : part.first + part.count, own_rows(part, side, q), :]
         return block.reshape(part.tiles * 8, 128)
 
-    for turn, part in enumerate(parts):
+    for third, part in enumerate(parts):
         term = lax.dot_general(
-            columns[64 * turn : 64 * turn + 512, :], dpre, TN, preferred_element_type=F32
-        )
-        terms[9 * turn : 9 * turn + 9] = term.reshape(9, 128, 128)
-        for d in far_first(part.n1) + [0]:
-            q = block_at(part, d)
-            part.pair_out[q] = my_term(part, 1 - core, q).astype(BF16)
-            pair_copy(part, q).start()
+            columns[64 * third : 64 * third + 512, :], dpre, TN, preferred_element_type=F32
+        )
+        terms[9 * third : 9 * third + 9] = term.reshape(9, 128, 128)
+        for run, (start, stop) in enumerate(part.pair_runs):
+            for turn in range(start, stop):
+                block = my_term(part, 1 - core, block_at(part, part.far1[turn]))
+                part.pair_out[turn] = block.astype(BF16)
+            pair_copy(part, run).start()
 
     def ring_copy(part, d):
         return remote(
@@ -301,19 +329,23 @@
             part.ring_send.at[d], part.ring_recv.at[d], peers[part.a1][d],
         )
 
-    def paired(part, q):
-        pair_copy(part, q).wait_recv()
-        return my_term(part, core, q) + part.pair_in[q].astype(F32)
-
-    orders = {part.index: far_first(part.n1) for part in parts}
-    for turn in range(max(len(order) for order in orders.values())):
+    def paired(part, turn):
+        for run, (start, stop) in enumerate(part.pair_runs):
+            if start == turn:
+                pair_copy(part, run).wait_recv()
+        own = my_term(part, core, block_at(part, part.far1[turn]))
+        return own + part.pair_in[turn].astype(F32)
+
+    if farthest >= 2:
+        await_word(farthest)
+    for turn in range(max(part.n1 for part in parts) - 1):
         for part in parts:
-            if turn < len(orders[part.index]):
-                d = orders[part.index][turn]
-                part.ring_out[d] = paired(part, block_at(part, d)).astype(BF16)
+            if turn < part.n1 - 1:
+                d = part.far1[turn]
+                part.ring_out[d] = paired(part, turn).astype(BF16)
                 ring_copy(part, d).start()
     for part in parts:
-        own = paired(part, block_at(part, 0))
+        own = paired(part, part.n1 - 1)
         part.mid[0 : part.tiles] = own.reshape(part.tiles, 8, 128)
         spare = part.per * part.n2 - part.tiles
         if spare:
@@ -361,95 +393,92 @@
         for d in reversed(far_first(part.n2)):
             mid_copy(part, d).wait_recv()
             block = block + part.mid_in[d]
+        block = block.reshape(part.per * 8, 128)
         part.row_out[...] = block
         for d in far_first(part.n3):
             row_copy(part, d).start()
         part.row_in[place[part.a3]] = block
 
     def thin_copy(part, slot):
-        home = part.full.at[core, place[part.a1]]
-        return remote(
-            home.at[0], home.at[slot],
+        return remote(
+            part.full.at[core, 0, 0], part.full.at[core, 0, slot],
             part.thin_send.at[slot], part.thin_recv.at[slot],
             peers[part.a2][part.near2[slot]],
         )
 
-    def wide_copy(part, group, d):
-        start, stop = part.groups[group]
-        block = part.full.at[core, place[part.a1], start:stop]
-        return remote(
-            block, block, part.wide_send.at[group, d], part.wide_recv.at[group, d],
-            peers[part.a1][d],
-        )
-
-    def core_copy(part, group, q):
-        start, stop = part.groups[group]
-        block = part.full.at[core, q, start:stop]
-        return remote(
-            block, block, part.core_send.at[group, q], part.core_recv.at[group, q], partner
-        )
-
-    for part in (parts[0], parts[1], parts[2]):
+    def wide_copy(part, slot):
+        return remote(
+            part.full.at[core, 0], part.full.at[core, slot],
+            part.wide_send.at[slot], part.wide_recv.at[slot],
+            peers[part.a1][part.near1[slot]],
+        )
+
+    def core_copy(part, run):
+        start, stop = part.core_runs[run]
+        block = part.full.at[core, start:stop]
+        return remote(
+            block, block, part.core_send.at[run], part.core_recv.at[run], partner
+        )
+
+    for part in parts:
         for d in reversed(far_first(part.n3)):
             row_copy(part, d).wait_recv()
         total = part.row_in[0]
         for x in range(1, part.n3):
             total = total + part.row_in[x]
-        part.full[core, place[part.a1], 0] = total.reshape(part.per * 8, 128).astype(BF16)
+        part.full[core, 0, 0] = total.astype(BF16)
         for slot in reversed(range(1, part.n2)):
             thin_copy(part, slot).start()
-
-    rounds = max(len(part.groups) for part in parts)
-    for group in range(rounds):
+    for part in parts:
+        for slot in range(1, part.n2):
+            thin_copy(part, slot).wait_recv()
+        for slot in reversed(range(1, part.n1)):
+            wide_copy(part, slot).start()
+    for run in range(max(len(part.core_runs) for part in parts)):
         for part in parts:
-            start, stop = part.groups[group]
-            for slot in range(max(start, 1), stop):
-                thin_copy(part, slot).wait_recv()
-            for d in far_first(part.n1):
-                wide_copy(part, group, d).start()
-            core_copy(part, group, block_at(part, 0)).start()
-    for group in range(rounds):
+            if run < len(part.core_runs):
+                start, stop = part.core_runs[run]
+                for slot in range(max(start, 1), stop):
+                    wide_copy(part, slot).wait_recv()
+                core_copy(part, run).start()
+
+    for other in range(2):
+        side = 1 - core if other else core
         for part in parts:
-            for d in reversed(far_first(part.n1)):
-                wide_copy(part, group, d).wait_recv()
-                core_copy(part, group, block_at(part, part.n1 - d)).start()
-
-    squares = jnp.zeros((8, 128), F32)
-    for part in parts:
-        where = [
-            (place[part.a2] + part.n2 - part.near2[slot]) % part.n2 for slot in range(part.n2)
-        ]
-        for step in range(2 * part.n1):
-            side, q = step // part.n1, step % part.n1
-            if side == 0:
-                side = core
-            else:
-                side = 1 - core
-                for group in range(len(part.groups)):
-                    core_copy(part, group, q).wait_recv()
-            for slot in range(part.n2):
-                piece = part.full[side, q, slot].astype(F32).reshape(part.per, 8, 128)
-                part.tiles_ref[pl.ds(where[slot] * part.per, part.per)] = piece
-            block = part.tiles_ref[0 : part.tiles]
-            squares = squares + jnp.sum(block * block, axis=0)
-            sum_ref[part.first : part.first + part.count, own_rows(part, side, q), :] = (
-                block.reshape(part.count, part.rows, 128)
-            )
+            if other:
+                for run in range(len(part.core_runs)):
+                    core_copy(part, run).wait_recv()
+            homes = [
+                (place[part.a2] + part.n2 - d) % part.n2 * part.per for d in part.near2
+            ]
+            for block_slot in range(part.n1):
+                for slot in range(part.n2):
+                    piece = part.full[side, block_slot, slot].astype(F32)
+                    part.tiles_ref[pl.ds(homes[slot], part.per)] = piece.reshape(
+                        part.per, 8, 128
+                    )
+                block = part.tiles_ref[0 : part.tiles]
+                q = block_at(part, part.n1 - part.near1[block_slot])
+                part.squares[side, q] = jnp.sum(block * block, axis=0)
+                rows = own_rows(part, side, q)
+                sum_ref[part.first : part.first + part.count, rows, :] = block.reshape(
+                    part.count, part.rows, 128
+                )
+    squares = sum(jnp.sum(part.squares[...], axis=(0, 1)) for part in parts)
     mean = jnp.full((8, 128), jnp.sum(squares) / (27 * 128 * 128), F32)
     norm_ref[...] = 1.0 / jnp.sqrt(mean + 1e-06)
 
     for turn in range(2):
         for index in range(8):
-            halo_copy(turn, index).wait_send()
+            pl.when(leads[index])(halo_copy(turn, index).wait_send)
     for part in parts:
-        for q in range(part.n1):
-            pair_copy(part, q).wait_send()
-            for group in range(len(part.groups)):
-                core_copy(part, group, q).wait_send()
+        for run in range(len(part.pair_runs)):
+            pair_copy(part, run).wait_send()
+        for run in range(len(part.core_runs)):
+            core_copy(part, run).wait_send()
         for d in range(1, part.n1):
             ring_copy(part, d).wait_send()
-            for group in range(len(part.groups)):
-                wide_copy(part, group, d).wait_send()
+            wide_copy(part, d).wait_send()
         for d in range(1, part.n2):
             mid_copy(part, d).wait_send()
             thin_copy(part, d).wait_send()
@@ -506,6 +535,7 @@
             pltpu.VMEM((2, 8, 64, 128), BF16),
             pltpu.VMEM((27, 128, 128), F32),
             dma((2, 8)), dma((2, 8)),
+            pltpu.SemaphoreType.REGULAR((2, 2, ring // 2 + 1)),
             *(shape for table in own for shape in table.values()),
         ],
         compiler_params=pltpu.CompilerParams(

time: 56.9 us -> 53.3 us (0.937)
  Pallas kernels: 56.1 us -> 52.6 us
    pallas_call x1, Pallas kernels: 54.8 us -> 51.2 us  [on_device(): pl.pallas_call(functools.partial(kernel, sizes, names), out_shape=(jax.Sh...]
where the time goes in v3:
time: 53.3 us; the launch traced here: 53.2 us
  Pallas kernels  52.6 us (99%)
  between operations  0.64 us (1%)
    pallas_call x1, Pallas kernels, on_device(): pl.pallas_call(functools.partial(kernel, sizes, names), out_shape=(jax.Sh...  51.2 us
    pallas_call x1, Pallas kernels, on_device(): pl.pallas_call(finish_kernel, out_shape=(jax.ShapeDtypeStruct((4, 128, 12...  1.33 us

profile of v3, /device:TPU:1, one launch (start us, length us, event | category | flops | bytes accessed | tf_op | source)
XLA Modules:
  0.0 53.2 jit_solution(16886323671590636765)
XLA Ops:
  0.6 51.2 %shard_map.86 = (bf16[4,128,128]{2,1,0:T(8,128)(2,1)S(1)}, f32[27,128,128]{2,1,0:T(8,128)S(1)}, f32[8,128]{1,0:T(8,128)S(1)}) custom-call(s32[4,27]{1,0:T(4,128)} %bitcast.3, s32[4,128]{1,0:T(4,128)} %refs_1_.1, bf16[4,128,128]{2,1,0:T(8,128)(2,1)} %refs_2_.1, s32[1,1024]{1,0:T(1,128)} %bitcast.2, bf16[27,128,128]{2,1,0:T(8,128)(2,1)} %refs_4_.1, ...), custom_call_target="tpu_custom_call" | custom-call | tf_op jit(solution)/shard_map/pallas_call | solution.py:517
  51.9 1.3 %shard_map.87 = (bf16[4,128,128]{2,1,0:T(8,128)(2,1)}, f32[27,128,128]{2,1,0:T(8,128)}) custom-call(bf16[4,128,128]{2,1,0:T(8,128)(2,1)S(1)} %get-tuple-element.5.grad_ref, f32[27,128,128]{2,1,0:T(8,128)S(1)} %get-tuple-element.6.sum_ref, f32[8,128]{1,0:T(8,128)S(1)} %get-tuple-element.7.norm_ref), custom_call_target="tpu_custom_call" | custom-call | tf_op jit(solution)/shard_map/pallas_call | solution.py:545

commit v4 on v3

--- a/solution.py
+++ b/solution.py
@@ -351,20 +351,6 @@
         if spare:
             part.mid[part.tiles :] = jnp.zeros((spare, 8, 128), F32)
 
-    take_halo(1)
-    fill_columns(columns_g, True)
-    back = jnp.zeros((512, 128), F32)
-    for q in range(3):
-        back += lax.dot_general(
-            columns_g[64 * (2 - q) : 64 * (2 - q) + 512, :], weight_t[q], NT,
-            preferred_element_type=F32,
-        )
-    back = (back * occ_cells[...].reshape(512, 128)).reshape(8, 8, 8, 128)
-    for slot in range(4):
-        i, j = slot // 2, slot % 2
-        block = back[4 * i : 4 * i + 4, 4 * j : 4 * j + 4]
-        grad_ref[slot] = block.reshape(128, 128).astype(BF16)
-
     def mid_copy(part, d):
         p = (place[part.a2] + d) % part.n2
         return remote(
@@ -381,6 +367,20 @@
         part.mid[0 : part.tiles] = block
         for d in far_first(part.n2):
             mid_copy(part, d).start()
+
+    take_halo(1)
+    fill_columns(columns_g, True)
+    back = jnp.zeros((512, 128), F32)
+    for q in range(3):
+        back += lax.dot_general(
+            columns_g[64 * (2 - q) : 64 * (2 - q) + 512, :], weight_t[q], NT,
+            preferred_element_type=F32,
+        )
+    back = (back * occ_cells[...].reshape(512, 128)).reshape(8, 8, 8, 128)
+    for slot in range(4):
+        i, j = slot // 2, slot % 2
+        block = back[4 * i : 4 * i + 4, 4 * j : 4 * j + 4]
+        grad_ref[slot] = block.reshape(128, 128).astype(BF16)
 
     def row_copy(part, d):
         return remote(

time: 53.3 us -> 53.3 us (level)
  no operation moved by 1% of the time
where the time goes in v4:
time: 53.3 us; the launch traced here: 53.2 us
  Pallas kernels  52.5 us (98%)
  between operations  0.64 us (1%)
    pallas_call x1, Pallas kernels, on_device(): pl.pallas_call(functools.partial(kernel, sizes, names), out_shape=(jax.Sh...  51.2 us
    pallas_call x1, Pallas kernels, on_device(): pl.pallas_call(finish_kernel, out_shape=(jax.ShapeDtypeStruct((4, 128, 12...  1.33 us

profile of v4, /device:TPU:1, one launch (start us, length us, event | category | flops | bytes accessed | tf_op | source)
XLA Modules:
  0.0 53.2 jit_solution(73300179865359055)
XLA Ops:
  0.6 51.2 %shard_map.86 = (bf16[4,128,128]{2,1,0:T(8,128)(2,1)S(1)}, f32[27,128,128]{2,1,0:T(8,128)S(1)}, f32[8,128]{1,0:T(8,128)S(1)}) custom-call(s32[4,27]{1,0:T(4,128)} %bitcast.3, s32[4,128]{1,0:T(4,128)} %refs_1_.1, bf16[4,128,128]{2,1,0:T(8,128)(2,1)} %refs_2_.1, s32[1,1024]{1,0:T(1,128)} %bitcast.2, bf16[27,128,128]{2,1,0:T(8,128)(2,1)} %refs_4_.1, ...), custom_call_target="tpu_custom_call" | custom-call | tf_op jit(solution)/shard_map/pallas_call | solution.py:517
  51.9 1.3 %shard_map.87 = (bf16[4,128,128]{2,1,0:T(8,128)(2,1)}, f32[27,128,128]{2,1,0:T(8,128)}) custom-call(bf16[4,128,128]{2,1,0:T(8,128)(2,1)S(1)} %get-tuple-element.5.grad_ref, f32[27,128,128]{2,1,0:T(8,128)S(1)} %get-tuple-element.6.sum_ref, f32[8,128]{1,0:T(8,128)S(1)} %get-tuple-element.7.norm_ref), custom_call_target="tpu_custom_call" | custom-call | tf_op jit(solution)/shard_map/pallas_call | solution.py:545
